TPU v7x, 32 devices: a whole 2x2x4 slice. The times are simulated.
32 devices in a mesh: blk: 8 (over z, x), grid: 4 (over y, core).
Axes of the slice: x: 2, y: 2, z: 4, core: 2. Of those that a mesh axis runs over, the one named last changes fastest.
Arguments:
- patches: bfloat16 [4, 1024, 1024], P('grid', 'blk'), may hold values from -6 to 6
- stem_weight: bfloat16 [2, 1024, 768], replicated, may hold values from -0.125 to 0.125
- norm_gain: bfloat16 [768], replicated, may hold values from 0.25 to 1.75
- w_qkv: bfloat16 [768, 1280], replicated, may hold values from -0.21875 to 0.21875
- w_out: bfloat16 [768, 768], replicated, may hold values from -0.21875 to 0.21875
- per_head_scale: float32 [12], replicated, may hold values from 0.05 to 1, as said below
- positions: int32 [1024], replicated, may hold values from 0 to 1023, each once
- d_out: bfloat16 [4, 1024, 768], P('grid', 'blk'), may hold values from -48 to 48
Outputs:
- d_stem_weight: float32 [2, 1024, 768], P(None, None, ('blk', 'grid'))
- d_norm_gain: float32 [768], P(('blk', 'grid'))
- d_w_qkv: float32 [768, 1280], P(('blk', 'grid'))
- d_w_out: float32 [768, 768], P(None, ('blk', 'grid'))
Inputs may be any that keep to these rules, and one draw needn't show every extreme that they name: A permutation of the 1024 positions of a band. `per_head_scale`: positive.
All inputs are finite; a program needn't handle non-finite values.
Results may differ from a plain program's by a relative error of at most 0.015.
The roundings to bfloat16 on the way count: a program that leaves them out, or rounds other values in their place, can miss the bound.
Values may be sent and summed in bfloat16 or wider, within the bound.
A program may use at most 128 MiB of HBM per device.

v0:
```python
from functools import partial

import jax
import jax.numpy as jnp
from jax import lax
from jax.experimental import pallas as pl
from jax.experimental.pallas import tpu as pltpu
from jax.sharding import PartitionSpec as P

QUERY_HEADS = 12
KEY_VALUE_HEADS = 4
HEAD_SIZE = 64
TC = 16


def shifted(x, axis, by):
    peers = lax.axis_size(axis)
    pairs = [(i, i + by) for i in range(peers) if 0 <= i + by < peers]
    return lax.ppermute(x, axis, pairs)


def passed_along(x, axis, by):
    peers = lax.axis_size(axis)
    return lax.ppermute(x, axis, [(i, (i + by) % peers) for i in range(peers)])


def row_norm(values):
    return values * lax.rsqrt(jnp.mean(values * values, axis=-1, keepdims=True) + 1e-05)


def head_norm(values):
    return values * lax.rsqrt(jnp.mean(values * values, axis=-1, keepdims=True) + 1e-06)


def log2(n):
    return n.bit_length() - 1


def halving_orders(grid_bits, blk_bits):
    y = list(range(grid_bits))
    low = list(range(grid_bits, grid_bits + blk_bits))
    rest = low[1:]
    return [y + rest[:1] + rest[1:] + low[:1], low[:1] + y + rest, rest[:1] + low[:1] + y + rest[1:]]


def chip_partner(bit, grid_bits, own_blk, own_grid):
    if bit < grid_bits:
        step = 2 << bit
        mine = own_grid // step % 2
        return {"blk": own_blk, "grid": own_grid + (1 - 2 * mine) * step}, mine
    step = 1 << (bit - grid_bits)
    mine = own_blk // step % 2
    return {"blk": own_blk + (1 - 2 * mine) * step, "grid": own_grid}, mine


def transposed_dot(a, b):
    return lax.dot_general(a, b, (((0,), (0,)), ((), ())), preferred_element_type=jnp.float32)


def rowwise_dot(a, b):
    return lax.dot_general(a, b, (((1,), (1,)), ((), ())), preferred_element_type=jnp.float32)


def plain_dot(a, b):
    return jnp.dot(a, b, preferred_element_type=jnp.float32)


def half_sums(x):
    low = lax.broadcasted_iota(jnp.int32, x.shape, 1) < HEAD_SIZE
    first = jnp.sum(jnp.where(low, x, 0.0), axis=1, keepdims=True)
    second = jnp.sum(jnp.where(low, 0.0, x), axis=1, keepdims=True)
    return jnp.where(low, first, second)


def layer_kernel(plan, *refs):
    nb, grid_bits, orders, widths, offsets = plan
    (scale_ref, tiles_ref, grad_ref, stem_hbm, gain_ref, wqkv_hbm, wout_hbm, pos_ref, result_ref) = refs[:9]
    scratch = list(refs[9:])
    parts = len(widths)
    first = [scratch.pop(0) for _ in range(parts)]
    recv = [[scratch.pop(0) for _ in range(nb)] for _ in range(parts)]
    send = [[None] + [scratch.pop(0) for _ in range(nb - 1)] for _ in range(parts)]
    keep = [[scratch.pop(0) for _ in range(nb - 1)] for _ in range(parts)]
    (final, final_recv, stem_w, wqkv, wout, image, grad_pair, hidden_pair, attn_pair, dqkv_pair, token_pair,
     kv, dkv_out, dkv_own, dkv_in, normed_ref, inv_ref, qk_ref, heads_inv, qn, da, attn, dq, dqkv,
     load_sem, pair_send, pair_got, halo_send, halo_got, kv_send, kv_got, dkv_send, dkv_got, send_sem, recv_sem) = scratch
    tok, width = grad_ref.shape
    halo = image.shape[0] - 2 * tok
    span = kv.shape[0] * 128
    group = QUERY_HEADS // KEY_VALUE_HEADS
    own_blk = lax.axis_index("blk")
    own_grid = lax.axis_index("grid")
    blk_count = lax.axis_size("blk")
    grid_count = lax.axis_size("grid")
    core = own_grid % 2
    other_core = {"blk": own_blk, "grid": own_grid + 1 - 2 * core}
    above = {"blk": own_blk, "grid": (own_grid + grid_count - 1) % grid_count}
    under = {"blk": own_blk, "grid": (own_grid + 1) % grid_count}

    def along(offset):
        return {"blk": (own_blk + offset + blk_count) % blk_count, "grid": own_grid}

    loads = [
        pltpu.make_async_copy(stem_hbm, stem_w, load_sem.at[0]),
        pltpu.make_async_copy(wqkv_hbm, wqkv, load_sem.at[1]),
        pltpu.make_async_copy(wout_hbm, wout, load_sem.at[2]),
    ]
    for load in loads:
        load.start()

    barrier = pltpu.get_barrier_semaphore()
    peers = [chip_partner(bit, grid_bits, own_blk, own_grid)[0] for bit in range(nb)]
    peers += [other_core, above, under] + [along(j) for j in (1, 2, 3, -1, -2, -3)]
    for peer in peers:
        pl.semaphore_signal(barrier, inc=1, device_id=peer, device_id_type=pl.DeviceIdType.MESH)
    pl.semaphore_wait(barrier, len(peers))

    def push(source, target, sems, got, device):
        copy = pltpu.make_async_remote_copy(
            src_ref=source, dst_ref=target, send_sem=sems, recv_sem=got, device_id=device, device_id_type=pl.DeviceIdType.MESH
        )
        copy.start()
        return copy

    def pair(which, source, target):
        return push(source, target, pair_send.at[which], pair_got.at[which], other_core)

    own_rows = pl.ds(pl.multiple_of(core * tok, tok), tok)
    halo_copy = push(tiles_ref.at[:halo], image.at[2 * tok :], halo_send, halo_got, above)

    loads[0].wait()
    stem = plain_dot(tiles_ref[...], stem_w[0])
    halo_copy.wait()

    @pl.when(own_grid == grid_count - 1)
    def _():
        image[2 * tok :] = jnp.zeros((halo, image.shape[1]), image.dtype)

    below = jnp.concatenate([tiles_ref[halo:], image[2 * tok :]], axis=0)
    stem = stem + plain_dot(below, stem_w[1])
    token_f = stem.astype(jnp.bfloat16).astype(jnp.float32)
    inv = lax.rsqrt(jnp.sum(token_f * token_f, axis=1, keepdims=True) / width + 1e-05)
    normed = token_f * inv
    normed_ref[...] = normed
    inv_ref[...] = jnp.broadcast_to(inv, inv_ref.shape)
    gain_f = gain_ref[...].astype(jnp.float32).reshape(1, width)
    hidden = (normed * gain_f).astype(jnp.bfloat16)
    hidden_pair[core] = hidden
    loads[1].wait()
    key_start = QUERY_HEADS * HEAD_SIZE
    value_start = key_start + span

    def normalize(x):
        scale = lax.rsqrt(half_sums(x * x) / HEAD_SIZE + 1e-06)
        return scale, (x * scale).astype(jnp.bfloat16)

    keys = plain_dot(hidden, wqkv[:, key_start:])
    kv_copies = []
    for u in range(span // 128):
        at = u * 128
        heads_inv[:, key_start + at : key_start + at + 128], kv[u, 0, :, :128] = normalize(keys[:, at : at + 128])
        kv[u, 0, :, 128:] = keys[:, span + at : span + at + 128].astype(jnp.bfloat16)
        kv_copies.append([push(kv.at[u, 0], kv.at[u, j], kv_send.at[u, j], kv_got.at[u, j], along(j)) for j in (3, 2, 1)])
    qk_ref[:, key_start:] = keys[:, :span]
    tiles_copy = pair(0, tiles_ref, image.at[own_rows])
    grad_copy = pair(1, grad_ref, grad_pair.at[core])
    hidden_copy = pair(2, hidden_pair.at[core], hidden_pair.at[core])
    image[own_rows] = tiles_ref[...]
    grad_pair[core] = grad_ref[...]
    queries = plain_dot(hidden, wqkv[:, :key_start])
    qk_ref[:, :key_start] = queries
    for at in range(0, key_start, 128):
        heads_inv[:, at : at + 128], qn[:, at : at + 128] = normalize(queries[:, at : at + 128])
    loads[2].wait()
    da[...] = rowwise_dot(grad_ref[...], wout[...]).astype(jnp.bfloat16)

    query_pos = pos_ref[pl.ds(own_blk, 1), :]
    seen = []
    for j in range(4):
        key_pos = pos_ref[pl.ds((own_blk + blk_count - j) % blk_count, 1), :]
        column = jnp.broadcast_to(key_pos, (tok, tok)).T
        seen.append(column <= query_pos)
    visible = jnp.concatenate([jnp.where(x, 1.0, 0.0) for x in seen], axis=0) > 0.5
    dkv_copies = []
    for g in range(KEY_VALUE_HEADS):
        u, low_lane = g // 2, g % 2 * HEAD_SIZE
        lanes = slice(low_lane, low_lane + HEAD_SIZE)
        value_lanes = slice(128 + low_lane, 128 + low_lane + HEAD_SIZE)
        if g % 2 == 0:
            for copy in kv_copies[u]:
                copy.wait()
        keys_g = kv[u, :, :, lanes].reshape(4 * tok, HEAD_SIZE)
        values_g = kv[u, :, :, value_lanes].reshape(4 * tok, HEAD_SIZE)
        heads = [slice((g * group + i) * HEAD_SIZE, (g * group + i + 1) * HEAD_SIZE) for i in range(group)]
        queries_g = jnp.concatenate([qn[:, h] for h in heads], axis=0)
        grads_g = jnp.concatenate([da[:, h] for h in heads], axis=0)
        scores = rowwise_dot(keys_g, queries_g)
        dprobs = rowwise_dot(values_g, grads_g)
        probs, low = [], []
        for i in range(group):
            s = jnp.where(visible, scores[:, i * tok : (i + 1) * tok] * scale_ref[g * group + i], -1e30)
            weights = jnp.where(visible, jnp.exp(s - jnp.max(s, axis=0, keepdims=True)), 0.0)
            p = weights * (1.0 / jnp.sum(weights, axis=0, keepdims=True))
            probs.append(p)
            low.append(p.astype(jnp.bfloat16))
        low_g = jnp.concatenate(low, axis=1)
        attn_t = transposed_dot(values_g, low_g)
        delta = jnp.sum(grads_g.astype(jnp.float32).T * attn_t, axis=0, keepdims=True)
        ds = []
        for i in range(group):
            cols = slice(i * tok, (i + 1) * tok)
            ds.append((scale_ref[g * group + i] * probs[i] * (dprobs[:, cols] - delta[:, cols])).astype(jnp.bfloat16))
        ds_g = jnp.concatenate(ds, axis=1)
        dq_g = transposed_dot(keys_g, ds_g).T
        attn_g = attn_t.T
        for i in range(group):
            attn[:, heads[i]] = attn_g[i * tok : (i + 1) * tok].astype(jnp.bfloat16)
            dq[:, heads[i]] = dq_g[i * tok : (i + 1) * tok]
        dkeys = plain_dot(ds_g, queries_g).reshape(4, tok, HEAD_SIZE)
        dvalues = plain_dot(low_g, grads_g).reshape(4, tok, HEAD_SIZE)
        dkv_own[u, :, lanes] = dkeys[0]
        dkv_own[u, :, value_lanes] = dvalues[0]
        for j in (1, 2, 3):
            dkv_out[u, j - 1, :, lanes] = dkeys[j].astype(jnp.bfloat16)
            dkv_out[u, j - 1, :, value_lanes] = dvalues[j].astype(jnp.bfloat16)
        if g % 2 == 1:
            for j in (3, 2, 1):
                dkv_copies.append(push(dkv_out.at[u, j - 1], dkv_in.at[u, j - 1], dkv_send.at[u, j - 1], dkv_got.at[u, j - 1], along(-j)))
    half_attn = attn.shape[1] // 2
    attn_copy = pair(3, attn.at[:, pl.ds(pl.multiple_of((1 - core) * half_attn, 128), half_attn)], attn_pair.at[core])
    attn_pair[core] = attn[:, pl.ds(pl.multiple_of(core * half_attn, 128), half_attn)]

    def pull(at, g):
        scale = heads_inv[:, at : at + 128]
        x = qk_ref[:, at : at + 128] * scale
        return (scale * (g - x * (half_sums(g * x) / HEAD_SIZE))).astype(jnp.bfloat16)

    for at in range(0, key_start, 128):
        dqkv[:, at : at + 128] = pull(at, dq[:, at : at + 128])

    finals = []
    copies = [None] * parts
    steps = [0] * parts
    done = [None] * parts

    def transfer(part, source):
        partner = chip_partner(orders[part][steps[part]], grid_bits, own_blk, own_grid)[0]
        copies[part] = push(source, recv[part][steps[part]], send_sem.at[part, steps[part]], recv_sem.at[part, steps[part]], partner)

    def begin(members, left, right, extra=None):
        product = transposed_dot(left.reshape(2 * tok, width), right).astype(jnp.bfloat16)
        if extra is not None:
            product = jnp.concatenate([product, extra], axis=1)
        at = 0
        for part in members:
            first[part][...] = product[:, at : at + widths[part]].reshape(first[part].shape)
            at += widths[part]
            mine = chip_partner(orders[part][0], grid_bits, own_blk, own_grid)[1]
            transfer(part, first[part].at[:, 1 - mine])

    def advance(part):
        step = steps[part]
        order = orders[part]
        copies[part].wait()
        held = recv[part][step]
        mine = chip_partner(order[step], grid_bits, own_blk, own_grid)[1]
        left_over = [b for b in range(nb) if b not in order[:step]]
        inner = first[part].shape[2]

        def total(i):
            if step == 0:
                return first[part][i // inner, mine, i % inner].astype(jnp.float32) + held[i // inner, i % inner].astype(jnp.float32)
            return keep[part][step - 1][i] + held[i].astype(jnp.float32)

        steps[part] = step + 1
        if step == nb - 1:
            value = total(0)
            half = value.shape[0] // 2
            final[0, :, offsets[part] : offsets[part] + widths[part]] = value[:half]
            final[1, :, offsets[part] : offsets[part] + widths[part]] = value[half:]
            cols = slice(offsets[part], offsets[part] + widths[part])
            finals.append(pair(6 + part, final.at[1 - core, :, cols], final_recv.at[:, cols]))
            return
        left_over.remove(order[step])
        place_next = 1 << left_over.index(order[step + 1])
        mine_next = chip_partner(order[step + 1], grid_bits, own_blk, own_grid)[1]
        count = 1 << (nb - 2 - step)
        for r in range(count):
            away = r // place_next * (2 * place_next) + (1 - mine_next) * place_next + r % place_next
            send[part][step + 1][r] = total(away).astype(jnp.bfloat16)
        transfer(part, send[part][step + 1])
        for r in range(count):
            here = r // place_next * (2 * place_next) + mine_next * place_next + r % place_next
            keep[part][step][r] = total(here)

    attn_parts, qkv_parts, stem_parts = (0, 1, 2), (3, 4, 5), (6, 7, 8)
    attn_copy.wait()
    grad_copy.wait()
    begin(attn_parts, grad_pair[...], attn_pair[...].reshape(2 * tok, half_attn))

    for copy in dkv_copies:
        copy.wait()
    for u in range(span // 128):
        total_kv = dkv_own[u]
        for j in range(3):
            total_kv = total_kv + dkv_in[u, j].astype(jnp.float32)
        at = key_start + u * 128
        dqkv[:, at : at + 128] = pull(at, total_kv[:, :128])
        dqkv[:, at + span : at + span + 128] = total_kv[:, 128:].astype(jnp.bfloat16)
    half_qkv = dqkv.shape[1] // 2
    dqkv_copy = pair(4, dqkv.at[:, pl.ds(pl.multiple_of((1 - core) * half_qkv, 128), half_qkv)], dqkv_pair.at[core])
    dqkv_pair[core] = dqkv[:, pl.ds(pl.multiple_of(core * half_qkv, 128), half_qkv)]
    d_hidden = rowwise_dot(dqkv[...], wqkv[...])
    normed = normed_ref[...]
    flow = d_hidden * gain_f
    inner_mean = jnp.sum(flow * normed, axis=1, keepdims=True) / width
    d_tokens = grad_ref[...].astype(jnp.float32) + inv_ref[:, :1] * (flow - normed * inner_mean)
    token_pair[core] = d_tokens.astype(jnp.bfloat16)
    token_copy = pair(5, token_pair.at[core], token_pair.at[core])
    gain_term = jnp.sum(d_hidden * normed, axis=0, keepdims=True)
    gain_tile = jnp.broadcast_to(gain_term, (128, width)).T.astype(jnp.bfloat16)
    hidden_copy.wait()
    dqkv_copy.wait()
    begin(qkv_parts, hidden_pair[...], dqkv_pair[...].reshape(2 * tok, half_qkv))
    token_copy.wait()
    tiles_copy.wait()
    begin(stem_parts, token_pair[...], image[pl.ds(pl.multiple_of(core * halo, halo), 2 * tok)], gain_tile)
    for _ in range(nb):
        for part in range(parts):
            if steps[part] < nb:
                advance(part)
    for copy in finals:
        copy.wait()
    result_ref[core] = final[core]
    result_ref[1 - core] = final_recv[...]


def unpack_kernel(offsets, result_ref, stem_out, gain_out, qkv_out, out_out):
    half_out, half_qkv, gain_at = out_out.shape[1] // 2, qkv_out.shape[1] // 2, offsets[6] + stem_out.shape[2]
    for source in range(2):
        out_out[:, source * half_out : (source + 1) * half_out] = result_ref[source, :, : offsets[3]]
        qkv_out[:, source * half_qkv : (source + 1) * half_qkv] = result_ref[source, :, offsets[3] : offsets[6]]
        stem_out[source] = result_ref[source, :, offsets[6] : gain_at]
    gain_sum = result_ref[0, :, gain_at:] + result_ref[1, :, gain_at:]
    square = jnp.concatenate([gain_sum, jnp.zeros((128 - gain_sum.shape[0], 128), jnp.float32)], axis=0).T
    gain_out[...] = square[:1, : gain_out.shape[1]]


def whole_layer(tiles, grad_out, stem_weight, norm_gain, w_qkv, w_out, per_head_scale, positions):
    blk_bits, grid_bits = log2(lax.axis_size("blk")), log2(lax.axis_size("grid")) - 1
    nb = blk_bits + grid_bits
    tok, width = grad_out.shape
    pin = tiles.shape[1]
    qd, span = QUERY_HEADS * HEAD_SIZE, KEY_VALUE_HEADS * HEAD_SIZE
    rows = width >> nb
    half_qkv = w_qkv.shape[1] // 2
    part_widths = []
    for amount in (qd // 2, half_qkv, pin + 128):
        piece = (amount // 3 + 127) // 128 * 128
        part_widths += [piece, piece, amount - 2 * piece]
    offsets = [sum(part_widths[:i]) for i in range(9)]
    grid_first, low = list(range(grid_bits)), list(range(grid_bits, nb))
    turned = [low[i:] + low[:i] for i in (0, 1, 1)]
    orders = halving_orders(grid_bits, blk_bits) * 3
    firsts, recvs, sends, keeps = [], [], [], []
    for order, w in zip(orders, part_widths):
        inner = 1 << order[0]
        outer = (1 << nb) // (2 * inner)
        firsts.append(pltpu.VMEM((outer, 2, inner, rows, w), jnp.bfloat16))
        recvs.append(pltpu.VMEM((outer, inner, rows, w), jnp.bfloat16))
        for step in range(1, nb):
            shape = (1 << (nb - 1 - step), rows, w)
            recvs.append(pltpu.VMEM(shape, jnp.bfloat16))
            sends.append(pltpu.VMEM(shape, jnp.bfloat16))
            keeps.append(pltpu.VMEM(shape, jnp.float32))
    total = sum(part_widths)
    bf, f32 = jnp.bfloat16, jnp.float32
    buffers = [
        ((2, rows // 2, total), f32),
        ((rows // 2, total), f32),
        (stem_weight.shape, bf),
        (w_qkv.shape, bf),
        (w_out.shape, bf),
        ((2 * tok + TC, pin), bf),
        ((2, tok, width), bf),
        ((2, tok, width), bf),
        ((2, tok, qd // 2), bf),
        ((2, tok, half_qkv), bf),
        ((2, tok, width), bf),
        ((span // 128, 4, tok, 256), bf),
        ((span // 128, 3, tok, 256), bf),
        ((span // 128, tok, 256), f32),
        ((span // 128, 3, tok, 256), bf),
        ((tok, width), f32),
        ((tok, 128), f32),
        ((tok, qd + span), f32),
        ((tok, qd + span), f32),
        ((tok, qd), bf),
        ((tok, qd), bf),
        ((tok, qd), bf),
        ((tok, qd), f32),
        ((tok, w_qkv.shape[1]), bf),
    ]
    dma = pltpu.SemaphoreType.DMA
    halves = span // 128
    vmem = pl.BlockSpec(memory_space=pltpu.VMEM)
    hbm = pl.BlockSpec(memory_space=pl.ANY)
    result = pl.pallas_call(
        partial(layer_kernel, (nb, grid_bits, orders, part_widths, offsets)),
        out_shape=jax.ShapeDtypeStruct((2, rows // 2, total), f32),
        in_specs=[pl.BlockSpec(memory_space=pltpu.SMEM), vmem, vmem, hbm, vmem, hbm, hbm, vmem],
        out_specs=vmem,
        scratch_shapes=firsts
        + recvs
        + sends
        + keeps
        + [pltpu.VMEM(shape, kind) for shape, kind in buffers]
        + [dma((3,)), dma((15,)), dma((15,)), dma, dma, dma((halves, 4)), dma((halves, 4)), dma((halves, 3)), dma((halves, 3)), dma((9, nb)), dma((9, nb))],
        compiler_params=pltpu.CompilerParams(collective_id=0, has_side_effects=True, vmem_limit_bytes=63000000),
    )(per_head_scale, tiles, grad_out, stem_weight, norm_gain, w_qkv, w_out, positions.reshape(-1, tok))
    return pl.pallas_call(
        partial(unpack_kernel, offsets),
        out_shape=[
            jax.ShapeDtypeStruct(shape, f32)
            for shape in ((2, rows // 2, pin), (1, rows // 2), (rows // 2, w_qkv.shape[1]), (rows // 2, qd))
        ],
        in_specs=[vmem],
        out_specs=[vmem] * 4,
    )(result)


def shards(patches, stem_weight, norm_gain, w_qkv, w_out, per_head_scale, positions, d_out):
    tiles = patches[0]
    grad_out = d_out[0]
    chips = lax.axis_size("blk") * lax.axis_size("grid") // 2
    if (grad_out.shape[1] // chips) % 16 == 0:
        d_stem, d_gain, d_qkv, d_out_t = whole_layer(
            tiles, grad_out, stem_weight, norm_gain, w_qkv, w_out, per_head_scale, positions
        )
        return (d_stem.transpose(0, 2, 1), d_gain.reshape(-1), d_qkv, d_out_t.T)
    token_rows = tiles.shape[0]
    group_factor = QUERY_HEADS // KEY_VALUE_HEADS
    query_span_width = QUERY_HEADS * HEAD_SIZE
    key_span_width = KEY_VALUE_HEADS * HEAD_SIZE
    arrived = shifted(tiles[:TC], "grid", -1)
    below = jnp.concatenate([tiles[TC:], arrived], axis=0)
    stem = jnp.dot(tiles, stem_weight[0], preferred_element_type=jnp.float32)
    stem = stem + jnp.dot(below, stem_weight[1], preferred_element_type=jnp.float32)
    token_f = lax.optimization_barrier(stem.astype(jnp.bfloat16)).astype(jnp.float32)
    gain_f = norm_gain.astype(jnp.float32)
    normed = row_norm(token_f)
    hidden = (normed * gain_f).astype(jnp.bfloat16)
    query_key_value = jnp.dot(hidden, w_qkv, preferred_element_type=jnp.float32)
    query = query_key_value[:, :query_span_width].reshape(token_rows, QUERY_HEADS, HEAD_SIZE)
    key = query_key_value[:, query_span_width : query_span_width + key_span_width].reshape(
        token_rows, KEY_VALUE_HEADS, HEAD_SIZE
    )
    query_normalized = head_norm(query).astype(jnp.bfloat16)
    key_n = head_norm(key).astype(jnp.bfloat16).reshape(token_rows, key_span_width)
    value = query_key_value[:, query_span_width + key_span_width :].astype(jnp.bfloat16)
    attention_gradient = jnp.dot(grad_out, w_out.T, preferred_element_type=jnp.float32).astype(
        jnp.bfloat16
    )
    kv_own = jnp.concatenate([key_n, value], axis=1)
    blk_count = lax.axis_size("blk")
    own_index = lax.axis_index("blk")
    blocks = [kv_own]
    for offset in range(1, 4):
        blocks.append(passed_along(kv_own, "blk", offset))
    causal_window = jnp.concatenate(blocks, axis=0)
    key_pos = jnp.concatenate(
        [
            lax.dynamic_slice_in_dim(
                positions, (own_index - offset) % blk_count * token_rows, token_rows
            )
            for offset in range(4)
        ]
    )
    query_pos = lax.dynamic_slice_in_dim(positions, own_index * token_rows, token_rows)
    visible = (key_pos[None, :] <= query_pos[:, None])[None]
    every_key = causal_window.shape[0]
    query_cube = query_normalized.reshape(token_rows, KEY_VALUE_HEADS, group_factor, HEAD_SIZE)
    gradient_cube = attention_gradient.reshape(token_rows, KEY_VALUE_HEADS, group_factor, HEAD_SIZE)
    key_cube = causal_window[:, :key_span_width].reshape(every_key, KEY_VALUE_HEADS, HEAD_SIZE)
    value_cube = causal_window[:, key_span_width:].reshape(every_key, KEY_VALUE_HEADS, HEAD_SIZE)
    score_scales = per_head_scale.reshape(KEY_VALUE_HEADS, group_factor)
    prob_list = []
    low_list = []
    attn_list = []
    for query_head_group in range(KEY_VALUE_HEADS):
        scale_col = score_scales[query_head_group][:, None, None]
        attention_scores = (
            jnp.einsum(
                "trd,sd->rts",
                query_cube[:, query_head_group],
                key_cube[:, query_head_group],
                preferred_element_type=jnp.float32,
            )
            * scale_col
        )
        attention_scores = jnp.where(visible, attention_scores, -1e30)
        top = jnp.max(attention_scores, axis=-1, keepdims=True)
        weights = jnp.where(visible, jnp.exp(attention_scores - top), 0.0)
        probs = weights / jnp.sum(weights, axis=-1, keepdims=True)
        probability_narrow = probs.astype(jnp.bfloat16)
        prob_list.append(probs)
        low_list.append(probability_narrow)
        attn_list.append(
            jnp.einsum(
                "rts,sd->trd",
                probability_narrow,
                value_cube[:, query_head_group],
                preferred_element_type=jnp.float32,
            )
        )
    attention_output = (
        jnp.stack(attn_list, axis=1).reshape(token_rows, query_span_width).astype(jnp.bfloat16)
    )
    dquery_list = []
    dkey_list = []
    dvalue_list = []
    for query_head_group in range(KEY_VALUE_HEADS):
        scale_col = score_scales[query_head_group][:, None, None]
        grad_group = gradient_cube[:, query_head_group]
        softmax_delta = jnp.sum(
            grad_group.astype(jnp.float32) * attn_list[query_head_group], axis=-1
        )
        probability_gradient = jnp.einsum(
            "trd,sd->rts",
            grad_group,
            value_cube[:, query_head_group],
            preferred_element_type=jnp.float32,
        )
        score_gradient = (
            scale_col
            * prob_list[query_head_group]
            * (probability_gradient - softmax_delta.T[:, :, None])
        ).astype(jnp.bfloat16)
        dquery_list.append(
            jnp.einsum(
                "rts,sd->trd",
                score_gradient,
                key_cube[:, query_head_group],
                preferred_element_type=jnp.float32,
            )
        )
        dkey_list.append(
            jnp.einsum(
                "rts,trd->sd",
                score_gradient,
                query_cube[:, query_head_group],
                preferred_element_type=jnp.float32,
            )
        )
        dvalue_list.append(
            jnp.einsum(
                "rts,trd->sd",
                low_list[query_head_group],
                grad_group,
                preferred_element_type=jnp.float32,
            )
        )
    query_gradient = jnp.stack(dquery_list, axis=1).reshape(token_rows, QUERY_HEADS, HEAD_SIZE)
    dkey_all = jnp.stack(dkey_list, axis=1).reshape(every_key, key_span_width)
    dvalue_all = jnp.stack(dvalue_list, axis=1).reshape(every_key, key_span_width)
    partial_terms = jnp.concatenate([dkey_all, dvalue_all], axis=1)
    pieces = [partial_terms[offset * token_rows : (offset + 1) * token_rows] for offset in range(4)]
    carried_state = pieces[0]
    for offset in (1, 2, 3):
        carried_state = carried_state + passed_along(pieces[offset], "blk", -offset)
    pull_query = jax.vjp(head_norm, query)[1]
    gather_key = jax.vjp(head_norm, key)[1]
    dq_full = pull_query(query_gradient)[0].reshape(token_rows, query_span_width)
    key_gradient_whole = gather_key(
        carried_state[:, :key_span_width].reshape(token_rows, KEY_VALUE_HEADS, HEAD_SIZE)
    )[0].reshape(token_rows, key_span_width)
    d_qkv = jnp.concatenate(
        [dq_full, key_gradient_whole, carried_state[:, key_span_width:]], axis=1
    ).astype(jnp.bfloat16)
    d_hidden = jnp.dot(d_qkv, w_qkv.T, preferred_element_type=jnp.float32)
    gain_term = jnp.sum(d_hidden * normed, axis=0)
    pull_tokens = jax.vjp(row_norm, token_f)[1]
    d_tokens = (grad_out.astype(jnp.float32) + pull_tokens(d_hidden * gain_f)[0]).astype(
        jnp.bfloat16
    )
    stem_term = jnp.stack(
        [
            jnp.dot(tiles.T, d_tokens, preferred_element_type=jnp.float32),
            jnp.dot(below.T, d_tokens, preferred_element_type=jnp.float32),
        ]
    )
    qkv_term = jnp.dot(hidden.T, d_qkv, preferred_element_type=jnp.float32)
    out_term = jnp.dot(attention_output.T, grad_out, preferred_element_type=jnp.float32)
    d_stem_weight = lax.psum_scatter(stem_term, ("blk", "grid"), scatter_dimension=2, tiled=True)
    d_norm_gain = lax.psum_scatter(gain_term, ("blk", "grid"), scatter_dimension=0, tiled=True)
    d_w_qkv = lax.psum_scatter(qkv_term, ("blk", "grid"), scatter_dimension=0, tiled=True)
    d_w_out = lax.psum_scatter(out_term, ("blk", "grid"), scatter_dimension=1, tiled=True)
    return (d_stem_weight, d_norm_gain, d_w_qkv, d_w_out)


def solution(mesh):
    placed = (P("grid", "blk", None), P(), P(), P(), P(), P(), P(), P("grid", "blk", None))
    return jax.shard_map(
        shards,
        mesh=mesh,
        in_specs=placed,
        out_specs=(
            P(None, None, ("blk", "grid")),
            P(("blk", "grid")),
            P(("blk", "grid"), None),
            P(None, ("blk", "grid")),
        ),
        check_vma=False,
    )
```

profile of v0, /device:TPU:0, one launch (start us, length us, event | category | flops | bytes accessed | tf_op | source)
XLA Modules:
  0.0 73.0 jit_solution(13892469987569341233)
XLA Ops:
  0.6 70.6 %shard_map.111.result_ref = f32[2,24,2176]{2,1,0:T(8,128)} custom-call(f32[12]{0:T(128)} %refs_0_.1, bf16[128,1024]{1,0:T(8,128)(2,1)} %bitcast.6, bf16[128,768]{1,0:T(8,128)(2,1)} %bitcast.7, bf16[2,1024,768]{2,1,0:T(8,128)(2,1)} %refs_3_.1, bf16[768]{0:T(1024)(128)(2,1)} %refs_4_.1, bf16[768,1280]{1,0:T(8,128)(2,1)} %refs_5_.1, bf16[768,768]{1,0:T(8,128)(2,1)} %refs_6_.1, ...), custom_call_target="tpu_custom_call" | custom-call | tf_op jit(solution)/shard_map/pallas_call | solution.py:408
  71.2 1.8 %shard_map.112 = (f32[2,24,1024]{2,1,0:T(8,128)}, f32[1,24]{1,0:T(1,128)}, f32[24,1280]{1,0:T(8,128)}, f32[24,768]{1,0:T(8,128)}) custom-call(f32[2,24,2176]{2,1,0:T(8,128)} %shard_map.111.result_ref), custom_call_target="tpu_custom_call" | custom-call | tf_op jit(solution)/shard_map/pallas_call | solution.py:421
where the time goes:
time: 73.2 us; the launch traced here: 73 us
  Pallas kernels  72.4 us (99%)
    pallas_call x1, Pallas kernels, whole_layer(): pl.pallas_call(partial(layer_kernel, (nb, grid_bits, orders, part_widths,...  70.6 us
    pallas_call x1, Pallas kernels, whole_layer(): pl.pallas_call(partial(unpack_kernel, offsets), out_shape=[jax.ShapeDtype...  1.76 us

commit v1 on v0

--- a/solution.py
+++ b/solution.py
@@ -32,27 +32,6 @@
     return values * lax.rsqrt(jnp.mean(values * values, axis=-1, keepdims=True) + 1e-06)
 
 
-def log2(n):
-    return n.bit_length() - 1
-
-
-def halving_orders(grid_bits, blk_bits):
-    y = list(range(grid_bits))
-    low = list(range(grid_bits, grid_bits + blk_bits))
-    rest = low[1:]
-    return [y + rest[:1] + rest[1:] + low[:1], low[:1] + y + rest, rest[:1] + low[:1] + y + rest[1:]]
-
-
-def chip_partner(bit, grid_bits, own_blk, own_grid):
-    if bit < grid_bits:
-        step = 2 << bit
-        mine = own_grid // step % 2
-        return {"blk": own_blk, "grid": own_grid + (1 - 2 * mine) * step}, mine
-    step = 1 << (bit - grid_bits)
-    mine = own_blk // step % 2
-    return {"blk": own_blk + (1 - 2 * mine) * step, "grid": own_grid}, mine
-
-
 def transposed_dot(a, b):
     return lax.dot_general(a, b, (((0,), (0,)), ((), ())), preferred_element_type=jnp.float32)
 
@@ -72,20 +51,33 @@
     return jnp.where(low, first, second)
 
 
+def fits_planes(width):
+    blocks, bands = lax.axis_size("blk"), lax.axis_size("grid")
+    devices = blocks * bands
+    return bands == 4 and blocks % 2 == 0 and blocks >= 4 and width % devices == 0 and (width // devices) % 8 == 0
+
+
 def layer_kernel(plan, *refs):
-    nb, grid_bits, orders, widths, offsets = plan
-    (scale_ref, tiles_ref, grad_ref, stem_hbm, gain_ref, wqkv_hbm, wout_hbm, pos_ref, result_ref) = refs[:9]
-    scratch = list(refs[9:])
-    parts = len(widths)
-    first = [scratch.pop(0) for _ in range(parts)]
-    recv = [[scratch.pop(0) for _ in range(nb)] for _ in range(parts)]
-    send = [[None] + [scratch.pop(0) for _ in range(nb - 1)] for _ in range(parts)]
-    keep = [[scratch.pop(0) for _ in range(nb - 1)] for _ in range(parts)]
-    (final, final_recv, stem_w, wqkv, wout, image, grad_pair, hidden_pair, attn_pair, dqkv_pair, token_pair,
+    nz, parts = plan
+    (scale_ref, tiles_hbm, grad_hbm, stem_hbm, gain_ref, wqkv_hbm, wout_hbm, pos_ref) = refs[:8]
+    (stem_out, gain_out, qkv_out, out_out) = refs[8:12]
+    scratch = list(refs[12:])
+    count = len(parts)
+    first = [scratch.pop(0) for _ in range(count)]
+    got_a = [scratch.pop(0) for _ in range(count)]
+    send_b = [scratch.pop(0) for _ in range(count)]
+    got_b = [scratch.pop(0) for _ in range(count)]
+    send_z = [scratch.pop(0) for _ in range(count)]
+    got_z = [scratch.pop(0) for _ in range(count)]
+    (final, final_recv, stem_w, wqkv, wout, image, halo_rows, grad_pair, hidden_pair, attn_pair, dq_pair, dkv_pair,
      kv, dkv_out, dkv_own, dkv_in, normed_ref, inv_ref, qk_ref, heads_inv, qn, da, attn, dq, dqkv,
-     load_sem, pair_send, pair_got, halo_send, halo_got, kv_send, kv_got, dkv_send, dkv_got, send_sem, recv_sem) = scratch
-    tok, width = grad_ref.shape
-    halo = image.shape[0] - 2 * tok
+     tok_out, tok_all, stem_send, stem_got, gain_own, gain_got, gain_plane, gain_z, gain_col,
+     load_sem, pair_send, pair_got, final_send, final_got, halo_send, halo_got, tile_send, tile_got, pass_send, pass_got,
+     kv_send, kv_got, dkv_send, dkv_got, part_send, part_got, z_send, z_got, tok_send, tok_got, gain_send, gain_arrived,
+     gain_z_send, gain_z_got, stem_sent, stem_arrived) = scratch
+    tok, width = grad_pair.shape[1:]
+    halo = halo_rows.shape[0]
+    pin = image.shape[2]
     span = kv.shape[0] * 128
     group = QUERY_HEADS // KEY_VALUE_HEADS
     own_blk = lax.axis_index("blk")
@@ -93,27 +85,39 @@
     blk_count = lax.axis_size("blk")
     grid_count = lax.axis_size("grid")
     core = own_grid % 2
+    own_y = own_grid // 2
+    own_x = own_blk % 2
+    own_z = own_blk // 2
+    rows = width // (blk_count * grid_count)
     other_core = {"blk": own_blk, "grid": own_grid + 1 - 2 * core}
     above = {"blk": own_blk, "grid": (own_grid + grid_count - 1) % grid_count}
-    under = {"blk": own_blk, "grid": (own_grid + 1) % grid_count}
+    plane = [(i, j) for i in range(2) for j in range(grid_count) if i + j > 0]
 
     def along(offset):
         return {"blk": (own_blk + offset + blk_count) % blk_count, "grid": own_grid}
 
+    def beside(i, j):
+        return {"blk": own_z * 2 + (own_x + i) % 2, "grid": (own_grid + j) % grid_count}
+
+    def level(k):
+        return {"blk": (own_z + k) % nz * 2 + own_x, "grid": own_grid}
+
+    own_rows = pl.ds(pl.multiple_of(own_grid * tok, tok), tok)
     loads = [
-        pltpu.make_async_copy(stem_hbm, stem_w, load_sem.at[0]),
-        pltpu.make_async_copy(wqkv_hbm, wqkv, load_sem.at[1]),
-        pltpu.make_async_copy(wout_hbm, wout, load_sem.at[2]),
+        pltpu.make_async_copy(tiles_hbm, image.at[own_x, own_rows], load_sem.at[0]),
+        pltpu.make_async_copy(stem_hbm.at[0], stem_w.at[0], load_sem.at[1]),
+        pltpu.make_async_copy(stem_hbm.at[1], stem_w.at[1], load_sem.at[2]),
+        pltpu.make_async_copy(wqkv_hbm, wqkv, load_sem.at[3]),
+        pltpu.make_async_copy(grad_hbm, grad_pair.at[core], load_sem.at[4]),
+        pltpu.make_async_copy(wout_hbm, wout, load_sem.at[5]),
     ]
+    barrier = pltpu.get_barrier_semaphore()
+    peers = [beside(i, j) for i, j in plane] + [level(k) for k in range(1, nz)] + [along(j) for j in (1, 2, 3, -1, -2, -3)]
+    for peer in peers:
+        pl.semaphore_signal(barrier, inc=1, device_id=peer, device_id_type=pl.DeviceIdType.MESH)
     for load in loads:
         load.start()
-
-    barrier = pltpu.get_barrier_semaphore()
-    peers = [chip_partner(bit, grid_bits, own_blk, own_grid)[0] for bit in range(nb)]
-    peers += [other_core, above, under] + [along(j) for j in (1, 2, 3, -1, -2, -3)]
-    for peer in peers:
-        pl.semaphore_signal(barrier, inc=1, device_id=peer, device_id_type=pl.DeviceIdType.MESH)
-    pl.semaphore_wait(barrier, len(peers))
+    image[:, grid_count * tok :] = jnp.zeros((2, halo, pin), image.dtype)
 
     def push(source, target, sems, got, device):
         copy = pltpu.make_async_remote_copy(
@@ -125,18 +129,27 @@
     def pair(which, source, target):
         return push(source, target, pair_send.at[which], pair_got.at[which], other_core)
 
-    own_rows = pl.ds(pl.multiple_of(core * tok, tok), tok)
-    halo_copy = push(tiles_ref.at[:halo], image.at[2 * tok :], halo_send, halo_got, above)
+    def tiles_to(slot, i, j):
+        mine = image.at[own_x, own_rows]
+        return push(mine, mine, tile_send.at[slot], tile_got.at[slot], beside(i, j))
 
     loads[0].wait()
-    stem = plain_dot(tiles_ref[...], stem_w[0])
+    pl.semaphore_wait(barrier, len(peers))
+    halo_copy = push(image.at[own_x, pl.ds(pl.multiple_of(own_grid * tok, tok), halo)], halo_rows, halo_send, halo_got, above)
+    tile_copies = [tiles_to(0, 0, 2)]
+    tile_pair = pair(0, image.at[own_x, own_rows], image.at[own_x, own_rows])
+
+    loads[1].wait()
+    tiles = image[own_x, own_rows]
+    stem = plain_dot(tiles, stem_w[0])
+    loads[2].wait()
     halo_copy.wait()
 
     @pl.when(own_grid == grid_count - 1)
     def _():
-        image[2 * tok :] = jnp.zeros((halo, image.shape[1]), image.dtype)
-
-    below = jnp.concatenate([tiles_ref[halo:], image[2 * tok :]], axis=0)
+        halo_rows[...] = jnp.zeros(halo_rows.shape, halo_rows.dtype)
+
+    below = jnp.concatenate([tiles[halo:], halo_rows[...]], axis=0)
     stem = stem + plain_dot(below, stem_w[1])
     token_f = stem.astype(jnp.bfloat16).astype(jnp.float32)
     inv = lax.rsqrt(jnp.sum(token_f * token_f, axis=1, keepdims=True) / width + 1e-05)
@@ -146,9 +159,8 @@
     gain_f = gain_ref[...].astype(jnp.float32).reshape(1, width)
     hidden = (normed * gain_f).astype(jnp.bfloat16)
     hidden_pair[core] = hidden
-    loads[1].wait()
+    loads[3].wait()
     key_start = QUERY_HEADS * HEAD_SIZE
-    value_start = key_start + span
 
     def normalize(x):
         scale = lax.rsqrt(half_sums(x * x) / HEAD_SIZE + 1e-06)
@@ -162,17 +174,18 @@
         kv[u, 0, :, 128:] = keys[:, span + at : span + at + 128].astype(jnp.bfloat16)
         kv_copies.append([push(kv.at[u, 0], kv.at[u, j], kv_send.at[u, j], kv_got.at[u, j], along(j)) for j in (3, 2, 1)])
     qk_ref[:, key_start:] = keys[:, :span]
-    tiles_copy = pair(0, tiles_ref, image.at[own_rows])
-    grad_copy = pair(1, grad_ref, grad_pair.at[core])
+    tile_copies.append(tiles_to(1, 1, 0))
+    tile_copies.append(tiles_to(2, 1, 2))
+    loads[4].wait()
+    grad_copy = pair(1, grad_pair.at[core], grad_pair.at[core])
     hidden_copy = pair(2, hidden_pair.at[core], hidden_pair.at[core])
-    image[own_rows] = tiles_ref[...]
-    grad_pair[core] = grad_ref[...]
     queries = plain_dot(hidden, wqkv[:, :key_start])
     qk_ref[:, :key_start] = queries
     for at in range(0, key_start, 128):
         heads_inv[:, at : at + 128], qn[:, at : at + 128] = normalize(queries[:, at : at + 128])
-    loads[2].wait()
-    da[...] = rowwise_dot(grad_ref[...], wout[...]).astype(jnp.bfloat16)
+    loads[5].wait()
+    grad_own = grad_pair[core]
+    da[...] = rowwise_dot(grad_own, wout[...]).astype(jnp.bfloat16)
 
     query_pos = pos_ref[pl.ds(own_blk, 1), :]
     seen = []
@@ -226,9 +239,13 @@
         if g % 2 == 1:
             for j in (3, 2, 1):
                 dkv_copies.append(push(dkv_out.at[u, j - 1], dkv_in.at[u, j - 1], dkv_send.at[u, j - 1], dkv_got.at[u, j - 1], along(-j)))
-    half_attn = attn.shape[1] // 2
-    attn_copy = pair(3, attn.at[:, pl.ds(pl.multiple_of((1 - core) * half_attn, 128), half_attn)], attn_pair.at[core])
-    attn_pair[core] = attn[:, pl.ds(pl.multiple_of(core * half_attn, 128), half_attn)]
+    half = key_start // 2
+
+    def half_of(start, amount, which):
+        return pl.ds(pl.multiple_of(start + which * amount, 128), amount)
+
+    attn_copy = pair(3, attn.at[:, half_of(0, half, 1 - core)], attn_pair.at[core])
+    attn_pair[core] = attn[:, half_of(0, half, core)]
 
     def pull(at, g):
         scale = heads_inv[:, at : at + 128]
@@ -237,66 +254,82 @@
 
     for at in range(0, key_start, 128):
         dqkv[:, at : at + 128] = pull(at, dq[:, at : at + 128])
-
+    dq_copy = pair(4, dqkv.at[:, half_of(0, half, 1 - core)], dq_pair.at[core])
+    dq_pair[core] = dqkv[:, half_of(0, half, core)]
+
+    rc = 2 * rows
+    coords = [(own_x, own_y), (own_y, own_x)]
+    partners = [[beside(1, 0), beside(0, 2)], [beside(0, 2), beside(1, 0)]]
+    part_copies = [None] * count
+    z_copies = [None] * count
     finals = []
-    copies = [None] * parts
-    steps = [0] * parts
-    done = [None] * parts
-
-    def transfer(part, source):
-        partner = chip_partner(orders[part][steps[part]], grid_bits, own_blk, own_grid)[0]
-        copies[part] = push(source, recv[part][steps[part]], send_sem.at[part, steps[part]], recv_sem.at[part, steps[part]], partner)
-
-    def begin(members, left, right, extra=None):
+    starts = [sum(w for _, _, w in parts[:p]) for p in range(count)]
+
+    def begin(members, left, right):
         product = transposed_dot(left.reshape(2 * tok, width), right).astype(jnp.bfloat16)
-        if extra is not None:
-            product = jnp.concatenate([product, extra], axis=1)
         at = 0
-        for part in members:
-            first[part][...] = product[:, at : at + widths[part]].reshape(first[part].shape)
-            at += widths[part]
-            mine = chip_partner(orders[part][0], grid_bits, own_blk, own_grid)[1]
-            transfer(part, first[part].at[:, 1 - mine])
-
-    def advance(part):
-        step = steps[part]
-        order = orders[part]
-        copies[part].wait()
-        held = recv[part][step]
-        mine = chip_partner(order[step], grid_bits, own_blk, own_grid)[1]
-        left_over = [b for b in range(nb) if b not in order[:step]]
-        inner = first[part].shape[2]
-
-        def total(i):
-            if step == 0:
-                return first[part][i // inner, mine, i % inner].astype(jnp.float32) + held[i // inner, i % inner].astype(jnp.float32)
-            return keep[part][step - 1][i] + held[i].astype(jnp.float32)
-
-        steps[part] = step + 1
-        if step == nb - 1:
-            value = total(0)
-            half = value.shape[0] // 2
-            final[0, :, offsets[part] : offsets[part] + widths[part]] = value[:half]
-            final[1, :, offsets[part] : offsets[part] + widths[part]] = value[half:]
-            cols = slice(offsets[part], offsets[part] + widths[part])
-            finals.append(pair(6 + part, final.at[1 - core, :, cols], final_recv.at[:, cols]))
-            return
-        left_over.remove(order[step])
-        place_next = 1 << left_over.index(order[step + 1])
-        mine_next = chip_partner(order[step + 1], grid_bits, own_blk, own_grid)[1]
-        count = 1 << (nb - 2 - step)
-        for r in range(count):
-            away = r // place_next * (2 * place_next) + (1 - mine_next) * place_next + r % place_next
-            send[part][step + 1][r] = total(away).astype(jnp.bfloat16)
-        transfer(part, send[part][step + 1])
-        for r in range(count):
-            here = r // place_next * (2 * place_next) + mine_next * place_next + r % place_next
-            keep[part][step][r] = total(here)
-
-    attn_parts, qkv_parts, stem_parts = (0, 1, 2), (3, 4, 5), (6, 7, 8)
+        for p in members:
+            order, w = parts[p][1:]
+            for a in range(2):
+                for b in range(2):
+                    for r in range(nz):
+                        row = ((r * 2 + a) * 2 + b) * rc
+                        piece = product[row : row + rc, at : at + w]
+                        if order == 0:
+                            first[p][a, r, b] = piece
+                        else:
+                            first[p][b, r, a] = piece
+            at += w
+            mine = coords[order][0]
+            part_copies[p] = push(first[p].at[1 - mine], got_a[p], part_send.at[p, 0], part_got.at[p, 0], partners[order][0])
+
+    def middle(p):
+        order = parts[p][1]
+        mine, then = coords[order]
+        part_copies[p].wait()
+        for r in range(nz):
+            total = first[p][mine, r, 1 - then].astype(jnp.float32) + got_a[p][r, 1 - then].astype(jnp.float32)
+            send_b[p][r] = total.astype(jnp.bfloat16)
+        part_copies[p] = push(send_b[p], got_b[p], part_send.at[p, 1], part_got.at[p, 1], partners[order][1])
+
+    def plane_total(p, r):
+        mine, then = coords[parts[p][1]]
+        near = first[p][mine, r, then].astype(jnp.float32) + got_a[p][r, then].astype(jnp.float32)
+        return near + got_b[p][r].astype(jnp.float32)
+
+    def across(p):
+        part_copies[p].wait()
+        for r in range(nz):
+            send_z[p][r] = plane_total(p, r).astype(jnp.bfloat16)
+        z_copies[p] = [
+            push(send_z[p].at[(own_z + k) % nz], got_z[p].at[k - 1], z_send.at[p, k - 1], z_got.at[p, k - 1], level(k))
+            for k in range(1, nz)
+        ]
+
+    def finish(p):
+        for copy in z_copies[p]:
+            copy.wait()
+        total = plane_total(p, own_z)
+        for k in range(nz - 1):
+            total = total + got_z[p][k].astype(jnp.float32)
+        cols = slice(starts[p], starts[p] + parts[p][2])
+        final[0, :, cols] = total[:rows]
+        final[1, :, cols] = total[rows:]
+        finals.append(push(final.at[1 - core, :, cols], final_recv.at[:, cols], final_send.at[p], final_got.at[p], other_core))
+
+    of_out, of_query, of_key = [[p for p in range(count) if parts[p][0] == m] for m in range(3)]
     attn_copy.wait()
     grad_copy.wait()
-    begin(attn_parts, grad_pair[...], attn_pair[...].reshape(2 * tok, half_attn))
+    begin(of_out, grad_pair[...], attn_pair[...].reshape(2 * tok, half))
+    dq_copy.wait()
+    hidden_copy.wait()
+    begin(of_query, hidden_pair[...], dq_pair[...].reshape(2 * tok, half))
+
+    passed = []
+    for slot, (i, j) in enumerate(((0, 2), (1, 0), (1, 2))):
+        tile_copies[slot].wait()
+        where = image.at[(own_x + i) % 2, pl.ds(pl.multiple_of((own_grid + j) % grid_count * tok, tok), tok)]
+        passed.append(push(where, where, pass_send.at[slot], pass_got.at[slot], other_core))
 
     for copy in dkv_copies:
         copy.wait()
@@ -307,86 +340,140 @@
         at = key_start + u * 128
         dqkv[:, at : at + 128] = pull(at, total_kv[:, :128])
         dqkv[:, at + span : at + span + 128] = total_kv[:, 128:].astype(jnp.bfloat16)
-    half_qkv = dqkv.shape[1] // 2
-    dqkv_copy = pair(4, dqkv.at[:, pl.ds(pl.multiple_of((1 - core) * half_qkv, 128), half_qkv)], dqkv_pair.at[core])
-    dqkv_pair[core] = dqkv[:, pl.ds(pl.multiple_of(core * half_qkv, 128), half_qkv)]
+    dkv_copy = pair(5, dqkv.at[:, half_of(key_start, span, 1 - core)], dkv_pair.at[core])
+    dkv_pair[core] = dqkv[:, half_of(key_start, span, core)]
     d_hidden = rowwise_dot(dqkv[...], wqkv[...])
     normed = normed_ref[...]
     flow = d_hidden * gain_f
     inner_mean = jnp.sum(flow * normed, axis=1, keepdims=True) / width
-    d_tokens = grad_ref[...].astype(jnp.float32) + inv_ref[:, :1] * (flow - normed * inner_mean)
-    token_pair[core] = d_tokens.astype(jnp.bfloat16)
-    token_copy = pair(5, token_pair.at[core], token_pair.at[core])
-    gain_term = jnp.sum(d_hidden * normed, axis=0, keepdims=True)
-    gain_tile = jnp.broadcast_to(gain_term, (128, width)).T.astype(jnp.bfloat16)
-    hidden_copy.wait()
-    dqkv_copy.wait()
-    begin(qkv_parts, hidden_pair[...], dqkv_pair[...].reshape(2 * tok, half_qkv))
-    token_copy.wait()
-    tiles_copy.wait()
-    begin(stem_parts, token_pair[...], image[pl.ds(pl.multiple_of(core * halo, halo), 2 * tok)], gain_tile)
-    for _ in range(nb):
-        for part in range(parts):
-            if steps[part] < nb:
-                advance(part)
+    d_tokens = grad_pair[core].astype(jnp.float32) + inv_ref[:, :1] * (flow - normed * inner_mean)
+    turned = d_tokens.T
+    for c in range(4 * 2):
+        pieces = [turned[(r * 8 + c) * rows : (r * 8 + c + 1) * rows] for r in range(nz)]
+        tok_out[c] = jnp.concatenate(pieces, axis=0).astype(jnp.bfloat16)
+    own_lanes = pl.ds(pl.multiple_of(own_grid * tok, tok), tok)
+    gain_own[...] = jnp.sum(d_hidden * normed, axis=0, keepdims=True)
+    tok_copies = []
+    for slot, (i, j) in enumerate(plane):
+        to_grid = (own_grid + j) % grid_count
+        goal = (own_x + i) % 2 * grid_count + to_grid
+        tok_copies.append(push(tok_out.at[goal], tok_all.at[own_x, :, own_lanes], tok_send.at[slot], tok_got.at[slot], beside(i, j)))
+    gain_copies = [
+        push(gain_own, gain_got.at[slot], gain_send.at[slot], gain_arrived.at[slot], beside(i, j)) for slot, (i, j) in enumerate(plane)
+    ]
+    tok_all[own_x, :, own_lanes] = tok_out[own_x * grid_count + own_grid]
+
+    for p in of_out + of_query:
+        middle(p)
+    dkv_copy.wait()
+    begin(of_key, hidden_pair[...], dkv_pair[...].reshape(2 * tok, span))
+    tile_pair.wait()
+    for copy in passed + tok_copies:
+        copy.wait()
+    chunks = stem_send.shape[0]
+    step = pin // chunks
+    stem_copies = []
+    for h in range(chunks):
+        cols = slice(h * step, (h + 1) * step)
+        straight = plain_dot(tok_all[0], image[0, : grid_count * tok, cols]) + plain_dot(tok_all[1], image[1, : grid_count * tok, cols])
+        lower = plain_dot(tok_all[0], image[0, halo:, cols]) + plain_dot(tok_all[1], image[1, halo:, cols])
+        for r in range(nz):
+            both = jnp.concatenate([straight[r * rows : (r + 1) * rows], lower[r * rows : (r + 1) * rows]], axis=0)
+            stem_send[h, r] = both.astype(jnp.bfloat16)
+        stem_copies.append(
+            [
+                push(stem_send.at[h, (own_z + k) % nz], stem_got.at[h, k - 1], stem_sent.at[h, k - 1], stem_arrived.at[h, k - 1], level(k))
+                for k in range(1, nz)
+            ]
+        )
+    for copy in gain_copies:
+        copy.wait()
+    gain_sum = gain_own[...]
+    for slot in range(len(plane)):
+        gain_sum = gain_sum + gain_got[slot]
+    gain_plane[...] = gain_sum
+    gain_z_copies = [
+        push(gain_plane, gain_z.at[k - 1], gain_z_send.at[k - 1], gain_z_got.at[k - 1], level(k)) for k in range(1, nz)
+    ]
+    for p in of_out + of_query:
+        across(p)
+    for p in of_key:
+        middle(p)
+    for p in of_key:
+        across(p)
+    for p in of_out + of_query:
+        finish(p)
+    for copy in gain_z_copies:
+        copy.wait()
+    gain_sum = gain_plane[...]
+    for k in range(nz - 1):
+        gain_sum = gain_sum + gain_z[k]
+    gain_col[...] = jnp.broadcast_to(gain_sum, (128, width)).T
+    own_gain = gain_col[pl.ds(pl.multiple_of((own_blk * grid_count + own_grid) * rows, 8), rows), :]
+    square = jnp.concatenate([own_gain, jnp.zeros((128 - rows, 128), jnp.float32)], axis=0).T
+    gain_out[...] = square[:1, :rows]
+    for p in of_key:
+        finish(p)
+    for h in range(chunks):
+        for copy in stem_copies[h]:
+            copy.wait()
+        total = stem_send[h, own_z].astype(jnp.float32)
+        for k in range(nz - 1):
+            total = total + stem_got[h, k].astype(jnp.float32)
+        cols = slice(h * step, (h + 1) * step)
+        stem_out[0, :, cols] = total[:rows]
+        stem_out[1, :, cols] = total[rows:]
     for copy in finals:
         copy.wait()
-    result_ref[core] = final[core]
-    result_ref[1 - core] = final_recv[...]
-
-
-def unpack_kernel(offsets, result_ref, stem_out, gain_out, qkv_out, out_out):
-    half_out, half_qkv, gain_at = out_out.shape[1] // 2, qkv_out.shape[1] // 2, offsets[6] + stem_out.shape[2]
-    for source in range(2):
-        out_out[:, source * half_out : (source + 1) * half_out] = result_ref[source, :, : offsets[3]]
-        qkv_out[:, source * half_qkv : (source + 1) * half_qkv] = result_ref[source, :, offsets[3] : offsets[6]]
-        stem_out[source] = result_ref[source, :, offsets[6] : gain_at]
-    gain_sum = result_ref[0, :, gain_at:] + result_ref[1, :, gain_at:]
-    square = jnp.concatenate([gain_sum, jnp.zeros((128 - gain_sum.shape[0], 128), jnp.float32)], axis=0).T
-    gain_out[...] = square[:1, : gain_out.shape[1]]
+    for source, which in ((final.at[core], core), (final_recv, 1 - core)):
+        out_out[:, half_of(0, half, which)] = source[:, :half]
+        qkv_out[:, half_of(0, half, which)] = source[:, half : 2 * half]
+        qkv_out[:, half_of(key_start, span, which)] = source[:, 2 * half :]
+
+
+def unpack_kernel(*refs):
+    half = len(refs) // 2
+    for source, target in zip(refs[:half], refs[half:]):
+        target[...] = source[...]
 
 
 def whole_layer(tiles, grad_out, stem_weight, norm_gain, w_qkv, w_out, per_head_scale, positions):
-    blk_bits, grid_bits = log2(lax.axis_size("blk")), log2(lax.axis_size("grid")) - 1
-    nb = blk_bits + grid_bits
+    blk_count, grid_count = lax.axis_size("blk"), lax.axis_size("grid")
+    nz = blk_count // 2
     tok, width = grad_out.shape
     pin = tiles.shape[1]
     qd, span = QUERY_HEADS * HEAD_SIZE, KEY_VALUE_HEADS * HEAD_SIZE
-    rows = width >> nb
-    half_qkv = w_qkv.shape[1] // 2
-    part_widths = []
-    for amount in (qd // 2, half_qkv, pin + 128):
-        piece = (amount // 3 + 127) // 128 * 128
-        part_widths += [piece, piece, amount - 2 * piece]
-    offsets = [sum(part_widths[:i]) for i in range(9)]
-    grid_first, low = list(range(grid_bits)), list(range(grid_bits, nb))
-    turned = [low[i:] + low[:i] for i in (0, 1, 1)]
-    orders = halving_orders(grid_bits, blk_bits) * 3
-    firsts, recvs, sends, keeps = [], [], [], []
-    for order, w in zip(orders, part_widths):
-        inner = 1 << order[0]
-        outer = (1 << nb) // (2 * inner)
-        firsts.append(pltpu.VMEM((outer, 2, inner, rows, w), jnp.bfloat16))
-        recvs.append(pltpu.VMEM((outer, inner, rows, w), jnp.bfloat16))
-        for step in range(1, nb):
-            shape = (1 << (nb - 1 - step), rows, w)
-            recvs.append(pltpu.VMEM(shape, jnp.bfloat16))
-            sends.append(pltpu.VMEM(shape, jnp.bfloat16))
-            keeps.append(pltpu.VMEM(shape, jnp.float32))
-    total = sum(part_widths)
+    rows = width // (blk_count * grid_count)
+    rc = 2 * rows
+    parts = []
+    for m, (amount, wide) in enumerate(((qd // 2, 0), (qd // 2, 1), (span, 0))):
+        large = (amount // 128 + 1) // 2 * 128
+        for order in range(2):
+            parts.append((m, order, large if order == wide else amount - large))
     bf, f32 = jnp.bfloat16, jnp.float32
-    buffers = [
-        ((2, rows // 2, total), f32),
-        ((rows // 2, total), f32),
+    grouped = [[], [], [], [], [], []]
+    for _, _, w in parts:
+        grouped[0].append(((2, nz, 2, rc, w), bf))
+        grouped[1].append(((nz, 2, rc, w), bf))
+        grouped[2].append(((nz, rc, w), bf))
+        grouped[3].append(((nz, rc, w), bf))
+        grouped[4].append(((nz, rc, w), bf))
+        grouped[5].append(((nz - 1, rc, w), bf))
+    total = sum(w for _, _, w in parts)
+    chunks = 2
+    buffers = sum(grouped, []) + [
+        ((2, rows, total), f32),
+        ((rows, total), f32),
         (stem_weight.shape, bf),
         (w_qkv.shape, bf),
         (w_out.shape, bf),
-        ((2 * tok + TC, pin), bf),
+        ((2, grid_count * tok + TC, pin), bf),
+        ((TC, pin), bf),
         ((2, tok, width), bf),
         ((2, tok, width), bf),
         ((2, tok, qd // 2), bf),
-        ((2, tok, half_qkv), bf),
-        ((2, tok, width), bf),
+        ((2, tok, qd // 2), bf),
+        ((2, tok, span), bf),
         ((span // 128, 4, tok, 256), bf),
         ((span // 128, 3, tok, 256), bf),
         ((span // 128, tok, 256), f32),
@@ -400,40 +487,43 @@
         ((tok, qd), bf),
         ((tok, qd), f32),
         ((tok, w_qkv.shape[1]), bf),
+        ((2 * grid_count, nz * rows, tok), bf),
+        ((2, nz * rows, grid_count * tok), bf),
+        ((chunks, nz, rc, pin // chunks), bf),
+        ((chunks, nz - 1, rc, pin // chunks), bf),
+        ((1, width), f32),
+        ((2 * grid_count - 1, 1, width), f32),
+        ((1, width), f32),
+        ((nz - 1, 1, width), f32),
+        ((width, 128), f32),
     ]
     dma = pltpu.SemaphoreType.DMA
-    halves = span // 128
+    halves, count, others = span // 128, len(parts), 2 * grid_count - 1
+    semaphores = [dma((6,)), dma((6,)), dma((6,)), dma((count,)), dma((count,)), dma, dma, dma((3,)), dma((3,)), dma((3,)), dma((3,))]
+    semaphores += [dma((halves, 4)), dma((halves, 4)), dma((halves, 3)), dma((halves, 3)), dma((count, 2)), dma((count, 2))]
+    semaphores += [dma((count, nz - 1)), dma((count, nz - 1)), dma((others,)), dma((others,)), dma((others,)), dma((others,))]
+    semaphores += [dma((nz - 1,)), dma((nz - 1,)), dma((chunks, nz - 1)), dma((chunks, nz - 1))]
     vmem = pl.BlockSpec(memory_space=pltpu.VMEM)
     hbm = pl.BlockSpec(memory_space=pl.ANY)
-    result = pl.pallas_call(
-        partial(layer_kernel, (nb, grid_bits, orders, part_widths, offsets)),
-        out_shape=jax.ShapeDtypeStruct((2, rows // 2, total), f32),
-        in_specs=[pl.BlockSpec(memory_space=pltpu.SMEM), vmem, vmem, hbm, vmem, hbm, hbm, vmem],
-        out_specs=vmem,
-        scratch_shapes=firsts
-        + recvs
-        + sends
-        + keeps
-        + [pltpu.VMEM(shape, kind) for shape, kind in buffers]
-        + [dma((3,)), dma((15,)), dma((15,)), dma, dma, dma((halves, 4)), dma((halves, 4)), dma((halves, 3)), dma((halves, 3)), dma((9, nb)), dma((9, nb))],
+    shapes = [
+        jax.ShapeDtypeStruct(shape, f32)
+        for shape in ((2, rows, pin), (1, rows), (rows, w_qkv.shape[1]), (rows, qd))
+    ]
+    results = pl.pallas_call(
+        partial(layer_kernel, (nz, parts)),
+        out_shape=shapes,
+        in_specs=[pl.BlockSpec(memory_space=pltpu.SMEM), hbm, hbm, hbm, vmem, hbm, hbm, vmem],
+        out_specs=[vmem] * 4,
+        scratch_shapes=[pltpu.VMEM(shape, kind) for shape, kind in buffers] + semaphores,
         compiler_params=pltpu.CompilerParams(collective_id=0, has_side_effects=True, vmem_limit_bytes=63000000),
     )(per_head_scale, tiles, grad_out, stem_weight, norm_gain, w_qkv, w_out, positions.reshape(-1, tok))
-    return pl.pallas_call(
-        partial(unpack_kernel, offsets),
-        out_shape=[
-            jax.ShapeDtypeStruct(shape, f32)
-            for shape in ((2, rows // 2, pin), (1, rows // 2), (rows // 2, w_qkv.shape[1]), (rows // 2, qd))
-        ],
-        in_specs=[vmem],
-        out_specs=[vmem] * 4,
-    )(result)
+    return pl.pallas_call(unpack_kernel, out_shape=shapes, in_specs=[vmem] * 4, out_specs=[vmem] * 4)(*results)
 
 
 def shards(patches, stem_weight, norm_gain, w_qkv, w_out, per_head_scale, positions, d_out):
     tiles = patches[0]
     grad_out = d_out[0]
-    chips = lax.axis_size("blk") * lax.axis_size("grid") // 2
-    if (grad_out.shape[1] // chips) % 16 == 0:
+    if fits_planes(grad_out.shape[1]):
         d_stem, d_gain, d_qkv, d_out_t = whole_layer(
             tiles, grad_out, stem_weight, norm_gain, w_qkv, w_out, per_head_scale, positions
         )

time: 73.2 us -> 69 us (0.943)
  Pallas kernels: 72.4 us -> 68.2 us
    pallas_call x2, Pallas kernels: 72.4 us -> 68.2 us  [the longest x1 66.4 us: whole_layer(): pl.pallas_call(partial(layer_kernel, (nz, parts)), out_shape=shapes, in_s...]
where the time goes in v1:
time: 69 us; the launch traced here: 68.8 us
  Pallas kernels  68.2 us (99%)
    pallas_call x1, Pallas kernels, whole_layer(): pl.pallas_call(partial(layer_kernel, (nz, parts)), out_shape=shapes, in_s...  66.4 us
    pallas_call x1, Pallas kernels, whole_layer(): pl.pallas_call(unpack_kernel, out_shape=shapes, in_specs=[vmem] * 4, out_...  1.8 us

profile of v1, /device:TPU:0, one launch (start us, length us, event | category | flops | bytes accessed | tf_op | source)
XLA Modules:
  0.0 68.8 jit_solution(13970956695154107443)
XLA Ops:
  0.6 66.4 %shard_map.111 = (f32[2,24,1024]{2,1,0:T(8,128)}, f32[1,24]{1,0:T(1,128)}, f32[24,1280]{1,0:T(8,128)}, f32[24,768]{1,0:T(8,128)}) custom-call(f32[12]{0:T(128)} %refs_0_.1, bf16[128,1024]{1,0:T(8,128)(2,1)} %bitcast.6, bf16[128,768]{1,0:T(8,128)(2,1)} %bitcast.7, bf16[2,1024,768]{2,1,0:T(8,128)(2,1)} %refs_3_.1, bf16[768]{0:T(1024)(128)(2,1)} %refs_4_.1, ...), custom_call_target="tpu_custom_call" | custom-call | tf_op jit(solution)/shard_map/pallas_call | solution.py:512
  67.0 1.8 %shard_map.112 = (f32[2,24,1024]{2,1,0:T(8,128)}, f32[1,24]{1,0:T(1,128)}, f32[24,1280]{1,0:T(8,128)}, f32[24,768]{1,0:T(8,128)}) custom-call(f32[2,24,1024]{2,1,0:T(8,128)} %get-tuple-element.12.refs_0_, f32[1,24]{1,0:T(1,128)} %get-tuple-element.13.refs_1_, f32[24,1280]{1,0:T(8,128)} %get-tuple-element.14.refs_2_, f32[24,768]{1,0:T(8,128)} %get-tuple-element.15.refs_3_), custom_call_target="tpu_custom_call" | custom-call | tf_op jit(solution)/shard_map/pallas_call | solution.py:520

commit v2 on v1

--- a/solution.py
+++ b/solution.py
@@ -54,7 +54,7 @@
 def fits_planes(width):
     blocks, bands = lax.axis_size("blk"), lax.axis_size("grid")
     devices = blocks * bands
-    return bands == 4 and blocks % 2 == 0 and blocks >= 4 and width % devices == 0 and (width // devices) % 8 == 0
+    return bands == 4 and blocks == 8 and width % devices == 0 and (width // devices) % 8 == 0
 
 
 def layer_kernel(plan, *refs):
@@ -69,9 +69,11 @@
     got_b = [scratch.pop(0) for _ in range(count)]
     send_z = [scratch.pop(0) for _ in range(count)]
     got_z = [scratch.pop(0) for _ in range(count)]
+    send_w = [scratch.pop(0) for _ in range(count)]
+    got_w = [scratch.pop(0) for _ in range(count)]
     (final, final_recv, stem_w, wqkv, wout, image, halo_rows, grad_pair, hidden_pair, attn_pair, dq_pair, dkv_pair,
-     kv, dkv_out, dkv_own, dkv_in, normed_ref, inv_ref, qk_ref, heads_inv, qn, da, attn, dq, dqkv,
-     tok_out, tok_all, stem_send, stem_got, gain_own, gain_got, gain_plane, gain_z, gain_col,
+     kv, dkv_out, dkv_own, dkv_in, dkv_mid, normed_ref, inv_ref, qk_ref, heads_inv, qn, da, attn, dq, dqkv,
+     tok_out, tok_all, stem_send, stem_got, stem_next, stem_last, gain_own, gain_got, gain_plane, gain_z, gain_col,
      load_sem, pair_send, pair_got, final_send, final_got, halo_send, halo_got, tile_send, tile_got, pass_send, pass_got,
      kv_send, kv_got, dkv_send, dkv_got, part_send, part_got, z_send, z_got, tok_send, tok_got, gain_send, gain_arrived,
      gain_z_send, gain_z_got, stem_sent, stem_arrived) = scratch
@@ -88,6 +90,7 @@
     own_y = own_grid // 2
     own_x = own_blk % 2
     own_z = own_blk // 2
+    z_low, z_high = own_z % 2, own_z // 2
     rows = width // (blk_count * grid_count)
     other_core = {"blk": own_blk, "grid": own_grid + 1 - 2 * core}
     above = {"blk": own_blk, "grid": (own_grid + grid_count - 1) % grid_count}
@@ -101,6 +104,9 @@
 
     def level(k):
         return {"blk": (own_z + k) % nz * 2 + own_x, "grid": own_grid}
+
+    z_near = {"blk": own_blk + (1 - 2 * z_low) * 2, "grid": own_grid}
+    z_far = {"blk": own_blk + (1 - 2 * z_high) * 4, "grid": own_grid}
 
     own_rows = pl.ds(pl.multiple_of(own_grid * tok, tok), tok)
     loads = [
@@ -136,7 +142,7 @@
     loads[0].wait()
     pl.semaphore_wait(barrier, len(peers))
     halo_copy = push(image.at[own_x, pl.ds(pl.multiple_of(own_grid * tok, tok), halo)], halo_rows, halo_send, halo_got, above)
-    tile_copies = [tiles_to(0, 0, 2)]
+    tile_copies = [tiles_to(0, 0, 2), tiles_to(1, 1, 0)]
     tile_pair = pair(0, image.at[own_x, own_rows], image.at[own_x, own_rows])
 
     loads[1].wait()
@@ -172,10 +178,10 @@
         at = u * 128
         heads_inv[:, key_start + at : key_start + at + 128], kv[u, 0, :, :128] = normalize(keys[:, at : at + 128])
         kv[u, 0, :, 128:] = keys[:, span + at : span + at + 128].astype(jnp.bfloat16)
-        kv_copies.append([push(kv.at[u, 0], kv.at[u, j], kv_send.at[u, j], kv_got.at[u, j], along(j)) for j in (3, 2, 1)])
+        kv_copies.append([push(kv.at[u, 0], kv.at[u, 2], kv_send.at[u, 0], kv_got.at[u, 2], along(2))])
+        slot = 1 + 2 * own_x
+        kv_copies[u].append(push(kv.at[u, 0], kv.at[u, slot], kv_send.at[u, 1], kv_got.at[u, slot], along(slot)))
     qk_ref[:, key_start:] = keys[:, :span]
-    tile_copies.append(tiles_to(1, 1, 0))
-    tile_copies.append(tiles_to(2, 1, 2))
     loads[4].wait()
     grad_copy = pair(1, grad_pair.at[core], grad_pair.at[core])
     hidden_copy = pair(2, hidden_pair.at[core], hidden_pair.at[core])
@@ -194,14 +200,29 @@
         column = jnp.broadcast_to(key_pos, (tok, tok)).T
         seen.append(column <= query_pos)
     visible = jnp.concatenate([jnp.where(x, 1.0, 0.0) for x in seen], axis=0) > 0.5
-    dkv_copies = []
+    for u in range(span // 128):
+        kv_copies[u][0].wait_recv()
+        slot = 3 - 2 * own_x
+        kv_copies[u].append(push(kv.at[u, 2], kv.at[u, slot], kv_send.at[u, 2], kv_got.at[u, slot], beside(1, 0)))
+
+    def combine(u):
+        side_copies[u].wait()
+        dkv_mid[u] = (dkv_out[u, 1].astype(jnp.float32) + dkv_in[u, 1].astype(jnp.float32)).astype(jnp.bfloat16)
+        dkv_copies.append(push(dkv_mid.at[u], dkv_in.at[u, 2], dkv_send.at[u, 2], dkv_got.at[u, 2], along(-2)))
+
+    dkv_copies, side_copies = [], []
     for g in range(KEY_VALUE_HEADS):
         u, low_lane = g // 2, g % 2 * HEAD_SIZE
         lanes = slice(low_lane, low_lane + HEAD_SIZE)
         value_lanes = slice(128 + low_lane, 128 + low_lane + HEAD_SIZE)
         if g % 2 == 0:
-            for copy in kv_copies[u]:
+            kv_copies[u][0].wait_send()
+            for copy in kv_copies[u][1:]:
                 copy.wait()
+        if g == 2:
+            tile_copies[1].wait()
+            near = image.at[1 - own_x, own_rows]
+            tile_copies.append(push(near, near, tile_send.at[2], tile_got.at[2], beside(0, 2)))
         keys_g = kv[u, :, :, lanes].reshape(4 * tok, HEAD_SIZE)
         values_g = kv[u, :, :, value_lanes].reshape(4 * tok, HEAD_SIZE)
         heads = [slice((g * group + i) * HEAD_SIZE, (g * group + i + 1) * HEAD_SIZE) for i in range(group)]
@@ -237,8 +258,11 @@
             dkv_out[u, j - 1, :, lanes] = dkeys[j].astype(jnp.bfloat16)
             dkv_out[u, j - 1, :, value_lanes] = dvalues[j].astype(jnp.bfloat16)
         if g % 2 == 1:
-            for j in (3, 2, 1):
-                dkv_copies.append(push(dkv_out.at[u, j - 1], dkv_in.at[u, j - 1], dkv_send.at[u, j - 1], dkv_got.at[u, j - 1], along(-j)))
+            side_copies.append(push(dkv_out.at[u, 2 * own_x], dkv_in.at[u, 1], dkv_send.at[u, 1], dkv_got.at[u, 1], beside(1, 0)))
+            direct = dkv_out.at[u, 2 - 2 * own_x]
+            dkv_copies.append(push(direct, dkv_in.at[u, 0], dkv_send.at[u, 0], dkv_got.at[u, 0], along(2 * own_x - 3)))
+        if g == 2:
+            combine(0)
     half = key_start // 2
 
     def half_of(start, amount, which):
@@ -261,7 +285,6 @@
     coords = [(own_x, own_y), (own_y, own_x)]
     partners = [[beside(1, 0), beside(0, 2)], [beside(0, 2), beside(1, 0)]]
     part_copies = [None] * count
-    z_copies = [None] * count
     finals = []
     starts = [sum(w for _, _, w in parts[:p]) for p in range(count)]
 
@@ -299,24 +322,27 @@
 
     def across(p):
         part_copies[p].wait()
-        for r in range(nz):
-            send_z[p][r] = plane_total(p, r).astype(jnp.bfloat16)
-        z_copies[p] = [
-            push(send_z[p].at[(own_z + k) % nz], got_z[p].at[k - 1], z_send.at[p, k - 1], z_got.at[p, k - 1], level(k))
-            for k in range(1, nz)
-        ]
+        for h in range(2):
+            send_z[p][h] = plane_total(p, 2 * h + 1 - z_low).astype(jnp.bfloat16)
+        part_copies[p] = push(send_z[p], got_z[p], z_send.at[p, 0], z_got.at[p, 0], z_near)
+
+    def near_total(p, h):
+        return plane_total(p, 2 * h + z_low) + got_z[p][h].astype(jnp.float32)
+
+    def beyond(p):
+        part_copies[p].wait()
+        send_w[p][...] = near_total(p, 1 - z_high).astype(jnp.bfloat16)
+        part_copies[p] = push(send_w[p], got_w[p], z_send.at[p, 1], z_got.at[p, 1], z_far)
 
     def finish(p):
-        for copy in z_copies[p]:
-            copy.wait()
-        total = plane_total(p, own_z)
-        for k in range(nz - 1):
-            total = total + got_z[p][k].astype(jnp.float32)
+        part_copies[p].wait()
+        total = near_total(p, z_high) + got_w[p][...].astype(jnp.float32)
         cols = slice(starts[p], starts[p] + parts[p][2])
         final[0, :, cols] = total[:rows]
         final[1, :, cols] = total[rows:]
         finals.append(push(final.at[1 - core, :, cols], final_recv.at[:, cols], final_send.at[p], final_got.at[p], other_core))
 
+    combine(1)
     of_out, of_query, of_key = [[p for p in range(count) if parts[p][0] == m] for m in range(3)]
     attn_copy.wait()
     grad_copy.wait()
@@ -325,9 +351,12 @@
     hidden_copy.wait()
     begin(of_query, hidden_pair[...], dq_pair[...].reshape(2 * tok, half))
 
+    for p in of_out:
+        middle(p)
     passed = []
     for slot, (i, j) in enumerate(((0, 2), (1, 0), (1, 2))):
-        tile_copies[slot].wait()
+        if slot != 1:
+            tile_copies[slot].wait()
         where = image.at[(own_x + i) % 2, pl.ds(pl.multiple_of((own_grid + j) % grid_count * tok, tok), tok)]
         passed.append(push(where, where, pass_send.at[slot], pass_got.at[slot], other_core))
 
@@ -335,7 +364,7 @@
         copy.wait()
     for u in range(span // 128):
         total_kv = dkv_own[u]
-        for j in range(3):
+        for j in (0, 2):
             total_kv = total_kv + dkv_in[u, j].astype(jnp.float32)
         at = key_start + u * 128
         dqkv[:, at : at + 128] = pull(at, total_kv[:, :128])
@@ -363,7 +392,9 @@
     ]
     tok_all[own_x, :, own_lanes] = tok_out[own_x * grid_count + own_grid]
 
-    for p in of_out + of_query:
+    for p in of_out:
+        across(p)
+    for p in of_query:
         middle(p)
     dkv_copy.wait()
     begin(of_key, hidden_pair[...], dkv_pair[...].reshape(2 * tok, span))
@@ -379,13 +410,17 @@
         lower = plain_dot(tok_all[0], image[0, halo:, cols]) + plain_dot(tok_all[1], image[1, halo:, cols])
         for r in range(nz):
             both = jnp.concatenate([straight[r * rows : (r + 1) * rows], lower[r * rows : (r + 1) * rows]], axis=0)
-            stem_send[h, r] = both.astype(jnp.bfloat16)
-        stem_copies.append(
-            [
-                push(stem_send.at[h, (own_z + k) % nz], stem_got.at[h, k - 1], stem_sent.at[h, k - 1], stem_arrived.at[h, k - 1], level(k))
-                for k in range(1, nz)
-            ]
-        )
+            stem_send[h, r % 2, r // 2] = both.astype(jnp.bfloat16)
+        stem_copies.append(push(stem_send.at[h, 1 - z_low], stem_got.at[h], stem_sent.at[h, 0], stem_arrived.at[h, 0], z_near))
+
+    def stem_near(h, k):
+        return stem_send[h, z_low, k].astype(jnp.float32) + stem_got[h, k].astype(jnp.float32)
+
+    def stem_beyond(h):
+        stem_copies[h].wait()
+        stem_next[h] = stem_near(h, 1 - z_high).astype(jnp.bfloat16)
+        stem_copies[h] = push(stem_next.at[h], stem_last.at[h], stem_sent.at[h, 1], stem_arrived.at[h, 1], z_far)
+
     for copy in gain_copies:
         copy.wait()
     gain_sum = gain_own[...]
@@ -395,12 +430,20 @@
     gain_z_copies = [
         push(gain_plane, gain_z.at[k - 1], gain_z_send.at[k - 1], gain_z_got.at[k - 1], level(k)) for k in range(1, nz)
     ]
-    for p in of_out + of_query:
+    for p in of_query:
         across(p)
+    for p in of_out:
+        beyond(p)
     for p in of_key:
         middle(p)
+    for h in range(chunks):
+        stem_beyond(h)
     for p in of_key:
         across(p)
+    for p in of_query:
+        beyond(p)
+    for p in of_key:
+        beyond(p)
     for p in of_out + of_query:
         finish(p)
     for copy in gain_z_copies:
@@ -415,11 +458,8 @@
     for p in of_key:
         finish(p)
     for h in range(chunks):
-        for copy in stem_copies[h]:
-            copy.wait()
-        total = stem_send[h, own_z].astype(jnp.float32)
-        for k in range(nz - 1):
-            total = total + stem_got[h, k].astype(jnp.float32)
+        stem_copies[h].wait()
+        total = stem_near(h, z_high) + stem_last[h].astype(jnp.float32)
         cols = slice(h * step, (h + 1) * step)
         stem_out[0, :, cols] = total[:rows]
         stem_out[1, :, cols] = total[rows:]
@@ -451,14 +491,16 @@
         for order in range(2):
             parts.append((m, order, large if order == wide else amount - large))
     bf, f32 = jnp.bfloat16, jnp.float32
-    grouped = [[], [], [], [], [], []]
+    grouped = [[] for _ in range(8)]
     for _, _, w in parts:
         grouped[0].append(((2, nz, 2, rc, w), bf))
         grouped[1].append(((nz, 2, rc, w), bf))
         grouped[2].append(((nz, rc, w), bf))
         grouped[3].append(((nz, rc, w), bf))
-        grouped[4].append(((nz, rc, w), bf))
-        grouped[5].append(((nz - 1, rc, w), bf))
+        grouped[4].append(((2, rc, w), bf))
+        grouped[5].append(((2, rc, w), bf))
+        grouped[6].append(((rc, w), bf))
+        grouped[7].append(((rc, w), bf))
     total = sum(w for _, _, w in parts)
     chunks = 2
     buffers = sum(grouped, []) + [
@@ -478,6 +520,7 @@
         ((span // 128, 3, tok, 256), bf),
         ((span // 128, tok, 256), f32),
         ((span // 128, 3, tok, 256), bf),
+        ((span // 128, tok, 256), bf),
         ((tok, width), f32),
         ((tok, 128), f32),
         ((tok, qd + span), f32),
@@ -489,8 +532,10 @@
         ((tok, w_qkv.shape[1]), bf),
         ((2 * grid_count, nz * rows, tok), bf),
         ((2, nz * rows, grid_count * tok), bf),
-        ((chunks, nz, rc, pin // chunks), bf),
-        ((chunks, nz - 1, rc, pin // chunks), bf),
+        ((chunks, 2, nz // 2, rc, pin // chunks), bf),
+        ((chunks, nz // 2, rc, pin // chunks), bf),
+        ((chunks, rc, pin // chunks), bf),
+        ((chunks, rc, pin // chunks), bf),
         ((1, width), f32),
         ((2 * grid_count - 1, 1, width), f32),
         ((1, width), f32),
@@ -500,9 +545,9 @@
     dma = pltpu.SemaphoreType.DMA
     halves, count, others = span // 128, len(parts), 2 * grid_count - 1
     semaphores = [dma((6,)), dma((6,)), dma((6,)), dma((count,)), dma((count,)), dma, dma, dma((3,)), dma((3,)), dma((3,)), dma((3,))]
-    semaphores += [dma((halves, 4)), dma((halves, 4)), dma((halves, 3)), dma((halves, 3)), dma((count, 2)), dma((count, 2))]
-    semaphores += [dma((count, nz - 1)), dma((count, nz - 1)), dma((others,)), dma((others,)), dma((others,)), dma((others,))]
-    semaphores += [dma((nz - 1,)), dma((nz - 1,)), dma((chunks, nz - 1)), dma((chunks, nz - 1))]
+    semaphores += [dma((halves, 3)), dma((halves, 4)), dma((halves, 3)), dma((halves, 3)), dma((count, 2)), dma((count, 2))]
+    semaphores += [dma((count, 2)), dma((count, 2)), dma((others,)), dma((others,)), dma((others,)), dma((others,))]
+    semaphores += [dma((nz - 1,)), dma((nz - 1,)), dma((chunks, 2)), dma((chunks, 2))]
     vmem = pl.BlockSpec(memory_space=pltpu.VMEM)
     hbm = pl.BlockSpec(memory_space=pl.ANY)
     shapes = [

time: 69 us -> 64 us (0.928)
  Pallas kernels: 68.2 us -> 63.1 us
    pallas_call x1, Pallas kernels: 66.4 us -> 61.3 us  [whole_layer(): pl.pallas_call(partial(layer_kernel, (nz, parts)), out_shape=shapes, in_s...]
where the time goes in v2:
time: 64 us; the launch traced here: 63.8 us
  Pallas kernels  63.1 us (99%)
  between operations  0.64 us (1%)
    pallas_call x1, Pallas kernels, whole_layer(): pl.pallas_call(partial(layer_kernel, (nz, parts)), out_shape=shapes, in_s...  61.3 us
    pallas_call x1, Pallas kernels, whole_layer(): pl.pallas_call(unpack_kernel, out_shape=shapes, in_specs=[vmem] * 4, out_...  1.8 us

profile of v2, /device:TPU:0, one launch (start us, length us, event | category | flops | bytes accessed | tf_op | source)
XLA Modules:
  0.0 63.8 jit_solution(18142509255690788233)
XLA Ops:
  0.6 61.3 %shard_map.111 = (f32[2,24,1024]{2,1,0:T(8,128)}, f32[1,24]{1,0:T(1,128)}, f32[24,1280]{1,0:T(8,128)}, f32[24,768]{1,0:T(8,128)}) custom-call(f32[12]{0:T(128)} %refs_0_.1, bf16[128,1024]{1,0:T(8,128)(2,1)} %bitcast.6, bf16[128,768]{1,0:T(8,128)(2,1)} %bitcast.7, bf16[2,1024,768]{2,1,0:T(8,128)(2,1)} %refs_3_.1, bf16[768]{0:T(1024)(128)(2,1)} %refs_4_.1, ...), custom_call_target="tpu_custom_call" | custom-call | tf_op jit(solution)/shard_map/pallas_call | solution.py:557
  62.0 1.8 %shard_map.112 = (f32[2,24,1024]{2,1,0:T(8,128)}, f32[1,24]{1,0:T(1,128)}, f32[24,1280]{1,0:T(8,128)}, f32[24,768]{1,0:T(8,128)}) custom-call(f32[2,24,1024]{2,1,0:T(8,128)} %get-tuple-element.12.refs_0_, f32[1,24]{1,0:T(1,128)} %get-tuple-element.13.refs_1_, f32[24,1280]{1,0:T(8,128)} %get-tuple-element.14.refs_2_, f32[24,768]{1,0:T(8,128)} %get-tuple-element.15.refs_3_), custom_call_target="tpu_custom_call" | custom-call | tf_op jit(solution)/shard_map/pallas_call | solution.py:565

commit v3 on v2

--- a/solution.py
+++ b/solution.py
@@ -51,10 +51,23 @@
     return jnp.where(low, first, second)
 
 
+DIRECT_KEYS = 1
+CHAINED = 2
+
+
 def fits_planes(width):
     blocks, bands = lax.axis_size("blk"), lax.axis_size("grid")
     devices = blocks * bands
     return bands == 4 and blocks == 8 and width % devices == 0 and (width // devices) % 8 == 0
+
+
+def chip_partner(bit, own_blk, own_grid):
+    if bit == 0:
+        mine = own_grid // 2
+        return {"blk": own_blk, "grid": own_grid + (1 - 2 * mine) * 2}, mine
+    step = 1 << (bit - 1)
+    mine = own_blk // step % 2
+    return {"blk": own_blk + (1 - 2 * mine) * step, "grid": own_grid}, mine
 
 
 def layer_kernel(plan, *refs):
@@ -63,24 +76,21 @@
     (stem_out, gain_out, qkv_out, out_out) = refs[8:12]
     scratch = list(refs[12:])
     count = len(parts)
+    nb = len(parts[0][1])
     first = [scratch.pop(0) for _ in range(count)]
-    got_a = [scratch.pop(0) for _ in range(count)]
-    send_b = [scratch.pop(0) for _ in range(count)]
-    got_b = [scratch.pop(0) for _ in range(count)]
-    send_z = [scratch.pop(0) for _ in range(count)]
-    got_z = [scratch.pop(0) for _ in range(count)]
-    send_w = [scratch.pop(0) for _ in range(count)]
-    got_w = [scratch.pop(0) for _ in range(count)]
+    recv = [[scratch.pop(0) for _ in range(nb)] for _ in range(count)]
+    send = [[None] + [scratch.pop(0) for _ in range(nb - 1)] for _ in range(count)]
+    keep = [[scratch.pop(0) for _ in range(nb - 1)] for _ in range(count)]
     (final, final_recv, stem_w, wqkv, wout, image, halo_rows, grad_pair, hidden_pair, attn_pair, dq_pair, dkv_pair,
-     kv, dkv_out, dkv_own, dkv_in, dkv_mid, normed_ref, inv_ref, qk_ref, heads_inv, qn, da, attn, dq, dqkv,
+     kv, dkv_out, dkv_own, dkv_in, dkv_mid, dkv_side, normed_ref, inv_ref, qk_ref, heads_inv, qn, da, attn, dq, dqkv,
      tok_out, tok_all, stem_send, stem_got, stem_next, stem_last, gain_own, gain_got, gain_plane, gain_z, gain_col,
      load_sem, pair_send, pair_got, final_send, final_got, halo_send, halo_got, tile_send, tile_got, pass_send, pass_got,
-     kv_send, kv_got, dkv_send, dkv_got, part_send, part_got, z_send, z_got, tok_send, tok_got, gain_send, gain_arrived,
+     kv_send, kv_got, dkv_send, dkv_got, part_send, part_got, tok_send, tok_got, gain_send, gain_arrived,
      gain_z_send, gain_z_got, stem_sent, stem_arrived) = scratch
     tok, width = grad_pair.shape[1:]
     halo = halo_rows.shape[0]
     pin = image.shape[2]
-    span = kv.shape[0] * 128
+    span = kv.shape[0] * HEAD_SIZE
     group = QUERY_HEADS // KEY_VALUE_HEADS
     own_blk = lax.axis_index("blk")
     own_grid = lax.axis_index("grid")
@@ -132,6 +142,11 @@
         copy.start()
         return copy
 
+    def all_of(ref, sems, got):
+        return pltpu.make_async_remote_copy(
+            src_ref=ref, dst_ref=ref, send_sem=sems, recv_sem=got, device_id=other_core, device_id_type=pl.DeviceIdType.MESH
+        )
+
     def pair(which, source, target):
         return push(source, target, pair_send.at[which], pair_got.at[which], other_core)
 
@@ -173,14 +188,31 @@
         return scale, (x * scale).astype(jnp.bfloat16)
 
     keys = plain_dot(hidden, wqkv[:, key_start:])
-    kv_copies = []
+    def kv_push(g, source, slot, which, device):
+        return push(kv.at[g, source], kv.at[g, slot], kv_send.at[which], kv_got.at[g, slot], device)
+
+    def kv_copy(g, slot, which):
+        return pltpu.make_async_remote_copy(
+            src_ref=kv.at[g, 0], dst_ref=kv.at[g, slot], send_sem=kv_send.at[which], recv_sem=kv_got.at[g, slot],
+            device_id=along(2), device_id_type=pl.DeviceIdType.MESH,
+        )
+
     for u in range(span // 128):
         at = u * 128
-        heads_inv[:, key_start + at : key_start + at + 128], kv[u, 0, :, :128] = normalize(keys[:, at : at + 128])
-        kv[u, 0, :, 128:] = keys[:, span + at : span + at + 128].astype(jnp.bfloat16)
-        kv_copies.append([push(kv.at[u, 0], kv.at[u, 2], kv_send.at[u, 0], kv_got.at[u, 2], along(2))])
-        slot = 1 + 2 * own_x
-        kv_copies[u].append(push(kv.at[u, 0], kv.at[u, slot], kv_send.at[u, 1], kv_got.at[u, slot], along(slot)))
+        heads_inv[:, key_start + at : key_start + at + 128], key_n = normalize(keys[:, at : at + 128])
+        value = keys[:, span + at : span + at + 128].astype(jnp.bfloat16)
+        for e in range(2):
+            g, lanes = 2 * u + e, slice(e * HEAD_SIZE, (e + 1) * HEAD_SIZE)
+            kv[g, 0] = jnp.concatenate([key_n[:, lanes], value[:, lanes]], axis=1)
+            kv_push(g, 0, 2, 0, along(2))
+            if g < DIRECT_KEYS:
+                kv_push(g, 0, 1 + 2 * own_x, 1, along(1 + 2 * own_x))
+            else:
+
+                @pl.when(own_x == 0)
+                def _():
+                    kv_push(g, 0, 1, 1, along(1))
+
     qk_ref[:, key_start:] = keys[:, :span]
     loads[4].wait()
     grad_copy = pair(1, grad_pair.at[core], grad_pair.at[core])
@@ -200,31 +232,62 @@
         column = jnp.broadcast_to(key_pos, (tok, tok)).T
         seen.append(column <= query_pos)
     visible = jnp.concatenate([jnp.where(x, 1.0, 0.0) for x in seen], axis=0) > 0.5
-    for u in range(span // 128):
-        kv_copies[u][0].wait_recv()
-        slot = 3 - 2 * own_x
-        kv_copies[u].append(push(kv.at[u, 2], kv.at[u, slot], kv_send.at[u, 2], kv_got.at[u, slot], beside(1, 0)))
-
-    def combine(u):
-        side_copies[u].wait()
-        dkv_mid[u] = (dkv_out[u, 1].astype(jnp.float32) + dkv_in[u, 1].astype(jnp.float32)).astype(jnp.bfloat16)
-        dkv_copies.append(push(dkv_mid.at[u], dkv_in.at[u, 2], dkv_send.at[u, 2], dkv_got.at[u, 2], along(-2)))
-
-    dkv_copies, side_copies = [], []
+    def pass_up(g):
+        kv_copy(g, 1, 3).wait_recv()
+
+        @pl.when(own_x == 0)
+        def _():
+            kv_push(g, 1, 3, 3, along(2))
+
     for g in range(KEY_VALUE_HEADS):
-        u, low_lane = g // 2, g % 2 * HEAD_SIZE
-        lanes = slice(low_lane, low_lane + HEAD_SIZE)
-        value_lanes = slice(128 + low_lane, 128 + low_lane + HEAD_SIZE)
-        if g % 2 == 0:
-            kv_copies[u][0].wait_send()
-            for copy in kv_copies[u][1:]:
-                copy.wait()
+        kv_copy(g, 2, 0).wait_recv()
+        kv_push(g, 2, 3 - 2 * own_x, 2, beside(1, 0))
+        if g > DIRECT_KEYS:
+            pass_up(g - 1)
+
+    def dkv_push(source, g, slot, which, device):
+        return push(source, dkv_in.at[g, slot], dkv_send.at[which], dkv_got.at[g, slot], device)
+
+    def dkv_copy_of(g, slot, which):
+        return pltpu.make_async_remote_copy(
+            src_ref=dkv_out.at[g, 0], dst_ref=dkv_in.at[g, slot], send_sem=dkv_send.at[which], recv_sem=dkv_got.at[g, slot],
+            device_id=along(2), device_id_type=pl.DeviceIdType.MESH,
+        )
+
+    def give(g):
+        if g < CHAINED:
+            dkv_push(dkv_out.at[g, 2 - 2 * own_x], g, 3 * own_x, 0, along(own_x - 2))
+        else:
+            dkv_push(dkv_out.at[g, 2 * own_x], g, 1, 1, beside(1, 0))
+            dkv_push(dkv_out.at[g, 2 - 2 * own_x], g, 0, 0, along(2 * own_x - 3))
+
+    def sideways(g):
+        @pl.when(own_x == 0)
+        def _():
+            dkv_copy_of(g, 0, 0).wait_recv()
+            dkv_side[g] = (dkv_out[g, 0].astype(jnp.float32) + dkv_in[g, 0].astype(jnp.float32)).astype(jnp.bfloat16)
+
+        @pl.when(own_x == 1)
+        def _():
+            dkv_side[g] = dkv_out[g, 2]
+
+        dkv_push(dkv_side.at[g], g, 1, 1, beside(1, 0))
+
+    def combine(g):
+        dkv_copy_of(g, 1, 1).wait_recv()
+        dkv_mid[g] = (dkv_out[g, 1].astype(jnp.float32) + dkv_in[g, 1].astype(jnp.float32)).astype(jnp.bfloat16)
+        dkv_push(dkv_mid.at[g], g, 2, 2, along(-2))
+
+    for g in range(KEY_VALUE_HEADS):
+        if g <= DIRECT_KEYS - 1 or g == KEY_VALUE_HEADS:
+            kv_copy(g, 1, 3).wait_recv()
+        kv_copy(g, 3, 2).wait_recv()
         if g == 2:
             tile_copies[1].wait()
             near = image.at[1 - own_x, own_rows]
             tile_copies.append(push(near, near, tile_send.at[2], tile_got.at[2], beside(0, 2)))
-        keys_g = kv[u, :, :, lanes].reshape(4 * tok, HEAD_SIZE)
-        values_g = kv[u, :, :, value_lanes].reshape(4 * tok, HEAD_SIZE)
+        keys_g = kv[g, :, :, :HEAD_SIZE].reshape(4 * tok, HEAD_SIZE)
+        values_g = kv[g, :, :, HEAD_SIZE:].reshape(4 * tok, HEAD_SIZE)
         heads = [slice((g * group + i) * HEAD_SIZE, (g * group + i + 1) * HEAD_SIZE) for i in range(group)]
         queries_g = jnp.concatenate([qn[:, h] for h in heads], axis=0)
         grads_g = jnp.concatenate([da[:, h] for h in heads], axis=0)
@@ -252,17 +315,16 @@
             dq[:, heads[i]] = dq_g[i * tok : (i + 1) * tok]
         dkeys = plain_dot(ds_g, queries_g).reshape(4, tok, HEAD_SIZE)
         dvalues = plain_dot(low_g, grads_g).reshape(4, tok, HEAD_SIZE)
-        dkv_own[u, :, lanes] = dkeys[0]
-        dkv_own[u, :, value_lanes] = dvalues[0]
+        dkv_own[g] = jnp.concatenate([dkeys[0], dvalues[0]], axis=1)
         for j in (1, 2, 3):
-            dkv_out[u, j - 1, :, lanes] = dkeys[j].astype(jnp.bfloat16)
-            dkv_out[u, j - 1, :, value_lanes] = dvalues[j].astype(jnp.bfloat16)
-        if g % 2 == 1:
-            side_copies.append(push(dkv_out.at[u, 2 * own_x], dkv_in.at[u, 1], dkv_send.at[u, 1], dkv_got.at[u, 1], beside(1, 0)))
-            direct = dkv_out.at[u, 2 - 2 * own_x]
-            dkv_copies.append(push(direct, dkv_in.at[u, 0], dkv_send.at[u, 0], dkv_got.at[u, 0], along(2 * own_x - 3)))
-        if g == 2:
-            combine(0)
+            dkv_out[g, j - 1] = jnp.concatenate([dkeys[j], dvalues[j]], axis=1).astype(jnp.bfloat16)
+        give(g)
+        if g == 0:
+            pass_up(KEY_VALUE_HEADS - 1)
+        if 0 <= g - 1 < CHAINED:
+            sideways(g - 1)
+        if g >= 2:
+            combine(g - 2)
     half = key_start // 2
 
     def half_of(start, amount, which):
@@ -281,94 +343,101 @@
     dq_copy = pair(4, dqkv.at[:, half_of(0, half, 1 - core)], dq_pair.at[core])
     dq_pair[core] = dqkv[:, half_of(0, half, core)]
 
-    rc = 2 * rows
-    coords = [(own_x, own_y), (own_y, own_x)]
-    partners = [[beside(1, 0), beside(0, 2)], [beside(0, 2), beside(1, 0)]]
-    part_copies = [None] * count
-    finals = []
+    copies = [None] * count
+    steps = [0] * count
     starts = [sum(w for _, _, w in parts[:p]) for p in range(count)]
+
+    def transfer(p, source):
+        partner = chip_partner(parts[p][1][steps[p]], own_blk, own_grid)[0]
+        copies[p] = push(source, recv[p][steps[p]], part_send.at[steps[p]], part_got.at[p, steps[p]], partner)
 
     def begin(members, left, right):
         product = transposed_dot(left.reshape(2 * tok, width), right).astype(jnp.bfloat16)
         at = 0
         for p in members:
             order, w = parts[p][1:]
-            for a in range(2):
-                for b in range(2):
-                    for r in range(nz):
-                        row = ((r * 2 + a) * 2 + b) * rc
-                        piece = product[row : row + rc, at : at + w]
-                        if order == 0:
-                            first[p][a, r, b] = piece
-                        else:
-                            first[p][b, r, a] = piece
+            first[p][...] = product[:, at : at + w].reshape(first[p].shape)
             at += w
-            mine = coords[order][0]
-            part_copies[p] = push(first[p].at[1 - mine], got_a[p], part_send.at[p, 0], part_got.at[p, 0], partners[order][0])
-
-    def middle(p):
-        order = parts[p][1]
-        mine, then = coords[order]
-        part_copies[p].wait()
-        for r in range(nz):
-            total = first[p][mine, r, 1 - then].astype(jnp.float32) + got_a[p][r, 1 - then].astype(jnp.float32)
-            send_b[p][r] = total.astype(jnp.bfloat16)
-        part_copies[p] = push(send_b[p], got_b[p], part_send.at[p, 1], part_got.at[p, 1], partners[order][1])
-
-    def plane_total(p, r):
-        mine, then = coords[parts[p][1]]
-        near = first[p][mine, r, then].astype(jnp.float32) + got_a[p][r, then].astype(jnp.float32)
-        return near + got_b[p][r].astype(jnp.float32)
-
-    def across(p):
-        part_copies[p].wait()
-        for h in range(2):
-            send_z[p][h] = plane_total(p, 2 * h + 1 - z_low).astype(jnp.bfloat16)
-        part_copies[p] = push(send_z[p], got_z[p], z_send.at[p, 0], z_got.at[p, 0], z_near)
-
-    def near_total(p, h):
-        return plane_total(p, 2 * h + z_low) + got_z[p][h].astype(jnp.float32)
-
-    def beyond(p):
-        part_copies[p].wait()
-        send_w[p][...] = near_total(p, 1 - z_high).astype(jnp.bfloat16)
-        part_copies[p] = push(send_w[p], got_w[p], z_send.at[p, 1], z_got.at[p, 1], z_far)
-
-    def finish(p):
-        part_copies[p].wait()
-        total = near_total(p, z_high) + got_w[p][...].astype(jnp.float32)
-        cols = slice(starts[p], starts[p] + parts[p][2])
-        final[0, :, cols] = total[:rows]
-        final[1, :, cols] = total[rows:]
-        finals.append(push(final.at[1 - core, :, cols], final_recv.at[:, cols], final_send.at[p], final_got.at[p], other_core))
-
-    combine(1)
+            if order[0] < 2:
+                launch(p)
+
+    def launch(p):
+        mine = chip_partner(parts[p][1][0], own_blk, own_grid)[1]
+        transfer(p, first[p].at[:, 1 - mine])
+
+    def advance(p):
+        step, order = steps[p], parts[p][1]
+        copies[p].wait_recv()
+        held = recv[p][step]
+        mine = chip_partner(order[step], own_blk, own_grid)[1]
+        left_over = [b for b in range(nb) if b not in order[:step]]
+        inner = first[p].shape[2]
+
+        def total(i):
+            if step == 0:
+                return first[p][i // inner, mine, i % inner].astype(jnp.float32) + held[i // inner, i % inner].astype(jnp.float32)
+            return keep[p][step - 1][i] + held[i].astype(jnp.float32)
+
+        steps[p] = step + 1
+        if step == nb - 1:
+            value = total(0)
+            cols = slice(starts[p], starts[p] + parts[p][2])
+            final[0, :, cols] = value[:rows]
+            final[1, :, cols] = value[rows:]
+            push(final.at[1 - core, :, cols], final_recv.at[:, cols], final_send, final_got, other_core)
+            return
+        left_over.remove(order[step])
+        place_next = 1 << left_over.index(order[step + 1])
+        mine_next = chip_partner(order[step + 1], own_blk, own_grid)[1]
+        amount = 1 << (nb - 2 - step)
+        for r in range(amount):
+            away = r // place_next * (2 * place_next) + (1 - mine_next) * place_next + r % place_next
+            send[p][step + 1][r] = total(away).astype(jnp.bfloat16)
+        transfer(p, send[p][step + 1])
+        for r in range(amount):
+            here = r // place_next * (2 * place_next) + mine_next * place_next + r % place_next
+            keep[p][step][r] = total(here)
+
+    def advance_all(members):
+        for p in members:
+            advance(p)
+
     of_out, of_query, of_key = [[p for p in range(count) if parts[p][0] == m] for m in range(3)]
     attn_copy.wait()
     grad_copy.wait()
     begin(of_out, grad_pair[...], attn_pair[...].reshape(2 * tok, half))
-    dq_copy.wait()
-    hidden_copy.wait()
-    begin(of_query, hidden_pair[...], dq_pair[...].reshape(2 * tok, half))
-
-    for p in of_out:
-        middle(p)
-    passed = []
+    for g in range(KEY_VALUE_HEADS - 2, KEY_VALUE_HEADS):
+        combine(g)
+    launch(of_out[2])
     for slot, (i, j) in enumerate(((0, 2), (1, 0), (1, 2))):
         if slot != 1:
             tile_copies[slot].wait()
         where = image.at[(own_x + i) % 2, pl.ds(pl.multiple_of((own_grid + j) % grid_count * tok, tok), tok)]
-        passed.append(push(where, where, pass_send.at[slot], pass_got.at[slot], other_core))
-
-    for copy in dkv_copies:
-        copy.wait()
+        push(where, where, pass_send, pass_got, other_core)
+
+    advance_all(of_out[:2])
+    for g in range(KEY_VALUE_HEADS):
+        if g < CHAINED:
+
+            @pl.when(own_x == 0)
+            def _():
+                dkv_copy_of(g, 3, 0).wait_recv()
+                dkv_own[g] += dkv_in[g, 3].astype(jnp.float32)
+
+        else:
+            dkv_copy_of(g, 0, 0).wait_recv()
+        dkv_copy_of(g, 2, 2).wait_recv()
     for u in range(span // 128):
-        total_kv = dkv_own[u]
-        for j in (0, 2):
-            total_kv = total_kv + dkv_in[u, j].astype(jnp.float32)
+        sums = []
+        for g in (2 * u, 2 * u + 1):
+            total_kv = dkv_own[g] + dkv_in[g, 2].astype(jnp.float32)
+            if g >= CHAINED:
+                total_kv = total_kv + dkv_in[g, 0].astype(jnp.float32)
+            sums.append(total_kv)
         at = key_start + u * 128
-        dqkv[:, at : at + 128] = pull(at, total_kv[:, :128])
-        dqkv[:, at + span : at + span + 128] = total_kv[:, 128:].astype(jnp.bfloat16)
+        dqkv[:, at : at + 128] = pull(at, jnp.concatenate([x[:, :HEAD_SIZE] for x in sums], axis=1))
+        d_value = jnp.concatenate([x[:, HEAD_SIZE:] for x in sums], axis=1)
+        dqkv[:, at + span : at + span + 128] = d_value.astype(jnp.bfloat16)
     dkv_copy = pair(5, dqkv.at[:, half_of(key_start, span, 1 - core)], dkv_pair.at[core])
     dkv_pair[core] = dqkv[:, half_of(key_start, span, core)]
     d_hidden = rowwise_dot(dqkv[...], wqkv[...])
@@ -382,25 +451,25 @@
         tok_out[c] = jnp.concatenate(pieces, axis=0).astype(jnp.bfloat16)
     own_lanes = pl.ds(pl.multiple_of(own_grid * tok, tok), tok)
     gain_own[...] = jnp.sum(d_hidden * normed, axis=0, keepdims=True)
-    tok_copies = []
-    for slot, (i, j) in enumerate(plane):
+    for i, j in plane:
         to_grid = (own_grid + j) % grid_count
         goal = (own_x + i) % 2 * grid_count + to_grid
-        tok_copies.append(push(tok_out.at[goal], tok_all.at[own_x, :, own_lanes], tok_send.at[slot], tok_got.at[slot], beside(i, j)))
-    gain_copies = [
-        push(gain_own, gain_got.at[slot], gain_send.at[slot], gain_arrived.at[slot], beside(i, j)) for slot, (i, j) in enumerate(plane)
-    ]
+        push(tok_out.at[goal], tok_all.at[own_x, :, own_lanes], tok_send, tok_got, beside(i, j))
+    for slot, (i, j) in enumerate(plane):
+        push(gain_own, gain_got.at[slot], gain_send, gain_arrived, beside(i, j))
     tok_all[own_x, :, own_lanes] = tok_out[own_x * grid_count + own_grid]
 
-    for p in of_out:
-        across(p)
-    for p in of_query:
-        middle(p)
+    dq_copy.wait()
+    hidden_copy.wait()
+    begin(of_query, hidden_pair[...], dq_pair[...].reshape(2 * tok, half))
+
+    advance_all(of_out[:2])
     dkv_copy.wait()
     begin(of_key, hidden_pair[...], dkv_pair[...].reshape(2 * tok, span))
+    advance(of_out[2])
     tile_pair.wait()
-    for copy in passed + tok_copies:
-        copy.wait()
+    all_of(image.at[0, : 3 * tok], pass_send, pass_got).wait()
+    all_of(tok_out.at[: len(plane)], tok_send, tok_got).wait()
     chunks = stem_send.shape[0]
     step = pin // chunks
     stem_copies = []
@@ -411,43 +480,30 @@
         for r in range(nz):
             both = jnp.concatenate([straight[r * rows : (r + 1) * rows], lower[r * rows : (r + 1) * rows]], axis=0)
             stem_send[h, r % 2, r // 2] = both.astype(jnp.bfloat16)
-        stem_copies.append(push(stem_send.at[h, 1 - z_low], stem_got.at[h], stem_sent.at[h, 0], stem_arrived.at[h, 0], z_near))
+        stem_copies.append(push(stem_send.at[h, 1 - z_low], stem_got.at[h], stem_sent.at[0], stem_arrived.at[h, 0], z_near))
 
     def stem_near(h, k):
         return stem_send[h, z_low, k].astype(jnp.float32) + stem_got[h, k].astype(jnp.float32)
 
     def stem_beyond(h):
-        stem_copies[h].wait()
+        stem_copies[h].wait_recv()
         stem_next[h] = stem_near(h, 1 - z_high).astype(jnp.bfloat16)
-        stem_copies[h] = push(stem_next.at[h], stem_last.at[h], stem_sent.at[h, 1], stem_arrived.at[h, 1], z_far)
-
-    for copy in gain_copies:
-        copy.wait()
+        stem_copies[h] = push(stem_next.at[h], stem_last.at[h], stem_sent.at[1], stem_arrived.at[h, 1], z_far)
+
+    all_of(gain_got, gain_send, gain_arrived).wait()
     gain_sum = gain_own[...]
     for slot in range(len(plane)):
         gain_sum = gain_sum + gain_got[slot]
     gain_plane[...] = gain_sum
-    gain_z_copies = [
-        push(gain_plane, gain_z.at[k - 1], gain_z_send.at[k - 1], gain_z_got.at[k - 1], level(k)) for k in range(1, nz)
-    ]
-    for p in of_query:
-        across(p)
-    for p in of_out:
-        beyond(p)
-    for p in of_key:
-        middle(p)
+    for k in range(1, nz):
+        push(gain_plane, gain_z.at[k - 1], gain_z_send, gain_z_got, level(k))
+    advance_all(of_query + of_out + of_key)
     for h in range(chunks):
         stem_beyond(h)
-    for p in of_key:
-        across(p)
-    for p in of_query:
-        beyond(p)
-    for p in of_key:
-        beyond(p)
-    for p in of_out + of_query:
-        finish(p)
-    for copy in gain_z_copies:
-        copy.wait()
+    advance_all(of_query + of_key + of_out[2:])
+    advance_all(of_query + of_out[:2] + of_key + of_out[2:])
+    advance_all(of_query)
+    all_of(gain_z, gain_z_send, gain_z_got).wait()
     gain_sum = gain_plane[...]
     for k in range(nz - 1):
         gain_sum = gain_sum + gain_z[k]
@@ -455,16 +511,33 @@
     own_gain = gain_col[pl.ds(pl.multiple_of((own_blk * grid_count + own_grid) * rows, 8), rows), :]
     square = jnp.concatenate([own_gain, jnp.zeros((128 - rows, 128), jnp.float32)], axis=0).T
     gain_out[...] = square[:1, :rows]
-    for p in of_key:
-        finish(p)
+    advance_all(of_key)
     for h in range(chunks):
-        stem_copies[h].wait()
+        stem_copies[h].wait_recv()
         total = stem_near(h, z_high) + stem_last[h].astype(jnp.float32)
         cols = slice(h * step, (h + 1) * step)
         stem_out[0, :, cols] = total[:rows]
         stem_out[1, :, cols] = total[rows:]
-    for copy in finals:
-        copy.wait()
+    all_of(final.at[0], final_send, final_got).wait()
+    all_of(kv.at[:, 0], kv_send.at[0], final_got).wait_send()
+    all_of(kv.at[:, 0], kv_send.at[2], final_got).wait_send()
+
+    @pl.when(own_x == 0)
+    def _():
+        all_of(kv.at[:, 0], kv_send.at[1], final_got).wait_send()
+        all_of(kv.at[DIRECT_KEYS:, 0], kv_send.at[3], final_got).wait_send()
+
+    @pl.when(own_x == 1)
+    def _():
+        all_of(kv.at[:DIRECT_KEYS, 0], kv_send.at[1], final_got).wait_send()
+
+    for which in range(3):
+        all_of(dkv_mid, dkv_send.at[which], final_got).wait_send()
+    for step in range(nb):
+        amount = count * (1 << (nb - 1 - step)) * 2 * rows * 128 // pin
+        all_of(image.at[0, :amount], part_send.at[step], final_got).wait_send()
+    all_of(stem_got, stem_sent.at[0], final_got).wait_send()
+    all_of(stem_last, stem_sent.at[1], final_got).wait_send()
     for source, which in ((final.at[core], core), (final_recv, 1 - core)):
         out_out[:, half_of(0, half, which)] = source[:, :half]
         qkv_out[:, half_of(0, half, which)] = source[:, half : 2 * half]
@@ -486,24 +559,24 @@
     rows = width // (blk_count * grid_count)
     rc = 2 * rows
     parts = []
-    for m, (amount, wide) in enumerate(((qd // 2, 0), (qd // 2, 1), (span, 0))):
-        large = (amount // 128 + 1) // 2 * 128
-        for order in range(2):
-            parts.append((m, order, large if order == wide else amount - large))
+    for m, orders in enumerate((((1, 0, 2, 3), (0, 1, 2, 3), (2, 1, 0, 3)), ((1, 0, 2, 3), (0, 1, 2, 3), (0, 1, 2, 3)), ((1, 0, 2, 3), (0, 1, 2, 3)))):
+        parts += [(m, order, 128) for order in orders]
+    nb = 4
     bf, f32 = jnp.bfloat16, jnp.float32
-    grouped = [[] for _ in range(8)]
-    for _, _, w in parts:
-        grouped[0].append(((2, nz, 2, rc, w), bf))
-        grouped[1].append(((nz, 2, rc, w), bf))
-        grouped[2].append(((nz, rc, w), bf))
-        grouped[3].append(((nz, rc, w), bf))
-        grouped[4].append(((2, rc, w), bf))
-        grouped[5].append(((2, rc, w), bf))
-        grouped[6].append(((rc, w), bf))
-        grouped[7].append(((rc, w), bf))
+    firsts, recvs, sends, keeps = [], [], [], []
+    for _, order, w in parts:
+        inner = 1 << order[0]
+        outer = (1 << nb) // (2 * inner)
+        firsts.append(((outer, 2, inner, rc, w), bf))
+        recvs.append(((outer, inner, rc, w), bf))
+        for step in range(1, nb):
+            shape = (1 << (nb - 1 - step), rc, w)
+            recvs.append((shape, bf))
+            sends.append((shape, bf))
+            keeps.append((shape, f32))
     total = sum(w for _, _, w in parts)
-    chunks = 2
-    buffers = sum(grouped, []) + [
+    chunks, heads = 4, KEY_VALUE_HEADS
+    buffers = firsts + recvs + sends + keeps + [
         ((2, rows, total), f32),
         ((rows, total), f32),
         (stem_weight.shape, bf),
@@ -516,11 +589,12 @@
         ((2, tok, qd // 2), bf),
         ((2, tok, qd // 2), bf),
         ((2, tok, span), bf),
-        ((span // 128, 4, tok, 256), bf),
-        ((span // 128, 3, tok, 256), bf),
-        ((span // 128, tok, 256), f32),
-        ((span // 128, 3, tok, 256), bf),
-        ((span // 128, tok, 256), bf),
+        ((heads, 4, tok, 2 * HEAD_SIZE), bf),
+        ((heads, 3, tok, 2 * HEAD_SIZE), bf),
+        ((heads, tok, 2 * HEAD_SIZE), f32),
+        ((heads, 4, tok, 2 * HEAD_SIZE), bf),
+        ((heads, tok, 2 * HEAD_SIZE), bf),
+        ((heads, tok, 2 * HEAD_SIZE), bf),
         ((tok, width), f32),
         ((tok, 128), f32),
         ((tok, qd + span), f32),
@@ -543,26 +617,32 @@
         ((width, 128), f32),
     ]
     dma = pltpu.SemaphoreType.DMA
-    halves, count, others = span // 128, len(parts), 2 * grid_count - 1
-    semaphores = [dma((6,)), dma((6,)), dma((6,)), dma((count,)), dma((count,)), dma, dma, dma((3,)), dma((3,)), dma((3,)), dma((3,))]
-    semaphores += [dma((halves, 3)), dma((halves, 4)), dma((halves, 3)), dma((halves, 3)), dma((count, 2)), dma((count, 2))]
-    semaphores += [dma((count, 2)), dma((count, 2)), dma((others,)), dma((others,)), dma((others,)), dma((others,))]
-    semaphores += [dma((nz - 1,)), dma((nz - 1,)), dma((chunks, 2)), dma((chunks, 2))]
+    count = len(parts)
+    semaphores = [dma((6,)), dma((6,)), dma((6,)), dma, dma, dma, dma, dma((3,)), dma((3,)), dma, dma]
+    semaphores += [dma((4,)), dma((heads, 4)), dma((3,)), dma((heads, 4)), dma((nb,)), dma((count, nb))]
+    semaphores += [dma] * 6 + [dma((2,)), dma((chunks, 2))]
     vmem = pl.BlockSpec(memory_space=pltpu.VMEM)
     hbm = pl.BlockSpec(memory_space=pl.ANY)
     shapes = [
         jax.ShapeDtypeStruct(shape, f32)
         for shape in ((2, rows, pin), (1, rows), (rows, w_qkv.shape[1]), (rows, qd))
     ]
+    inputs = (per_head_scale, tiles, grad_out, stem_weight, norm_gain, w_qkv, w_out, positions.reshape(-1, tok))
     results = pl.pallas_call(
         partial(layer_kernel, (nz, parts)),
         out_shape=shapes,
         in_specs=[pl.BlockSpec(memory_space=pltpu.SMEM), hbm, hbm, hbm, vmem, hbm, hbm, vmem],
         out_specs=[vmem] * 4,
         scratch_shapes=[pltpu.VMEM(shape, kind) for shape, kind in buffers] + semaphores,
-        compiler_params=pltpu.CompilerParams(collective_id=0, has_side_effects=True, vmem_limit_bytes=63000000),
-    )(per_head_scale, tiles, grad_out, stem_weight, norm_gain, w_qkv, w_out, positions.reshape(-1, tok))
-    return pl.pallas_call(unpack_kernel, out_shape=shapes, in_specs=[vmem] * 4, out_specs=[vmem] * 4)(*results)
+        compiler_params=pltpu.CompilerParams(collective_id=0, has_side_effects=True, vmem_limit_bytes=56000000),
+    )(*[pltpu.with_memory_space_constraint(value, pltpu.HBM) for value in inputs])
+    return pl.pallas_call(
+        unpack_kernel,
+        out_shape=shapes,
+        in_specs=[vmem] * 4,
+        out_specs=[vmem] * 4,
+        compiler_params=pltpu.CompilerParams(vmem_limit_bytes=4000000),
+    )(*results)
 
 
 def shards(patches, stem_weight, norm_gain, w_qkv, w_out, per_head_scale, positions, d_out):

time: 64 us -> 60.7 us (0.948)
  Pallas kernels: 63.1 us -> 59.9 us
    pallas_call x1, Pallas kernels: 61.3 us -> 59.2 us  [whole_layer(): pl.pallas_call(partial(layer_kernel, (nz, parts)), out_shape=shapes, in_s...]
    pallas_call x1, Pallas kernels: 1.8 us -> 0.77 us  [whole_layer(): pl.pallas_call(unpack_kernel, out_shape=shapes, in_specs=[vmem] * 4, out_...]
where the time goes in v3:
time: 60.7 us; the launch traced here: 60.6 us
  Pallas kernels  59.9 us (99%)
  between operations  0.64 us (1%)
    pallas_call x1, Pallas kernels, whole_layer(): pl.pallas_call(partial(layer_kernel, (nz, parts)), out_shape=shapes, in_s...  59.2 us

profile of v3, /device:TPU:0, one launch (start us, length us, event | category | flops | bytes accessed | tf_op | source)
XLA Modules:
  0.0 60.6 jit_solution(6711663677182029193)
XLA Ops:
  0.6 59.2 %shard_map.111 = (f32[2,24,1024]{2,1,0:T(8,128)S(1)}, f32[1,24]{1,0:T(1,128)S(1)}, f32[24,1280]{1,0:T(8,128)S(1)}, f32[24,768]{1,0:T(8,128)S(1)}) custom-call(f32[12]{0:T(128)} %refs_0_.1, bf16[128,1024]{1,0:T(8,128)(2,1)} %bitcast.6, bf16[128,768]{1,0:T(8,128)(2,1)} %bitcast.7, bf16[2,1024,768]{2,1,0:T(8,128)(2,1)} %refs_3_.1, bf16[768]{0:T(1024)(128)(2,1)} %refs_4_.1, ...), custom_call_target="tpu_custom_call" | custom-call | tf_op jit(solution)/shard_map/pallas_call | solution.py:631
  59.8 0.8 %shard_map.112 = (f32[2,24,1024]{2,1,0:T(8,128)}, f32[1,24]{1,0:T(1,128)}, f32[24,1280]{1,0:T(8,128)}, f32[24,768]{1,0:T(8,128)}) custom-call(f32[2,24,1024]{2,1,0:T(8,128)S(1)} %get-tuple-element.12.refs_0_, f32[1,24]{1,0:T(1,128)S(1)} %get-tuple-element.13.refs_1_, f32[24,1280]{1,0:T(8,128)S(1)} %get-tuple-element.14.refs_2_, ...), custom_call_target="tpu_custom_call" | custom-call | tf_op jit(solution)/shard_map/pallas_call | solution.py:639

commit v4 on v3

--- a/solution.py
+++ b/solution.py
@@ -51,7 +51,7 @@
     return jnp.where(low, first, second)
 
 
-DIRECT_KEYS = 1
+DIRECT_KEYS = 2
 CHAINED = 2
 
 
@@ -72,19 +72,19 @@
 
 def layer_kernel(plan, *refs):
     nz, parts = plan
-    (scale_ref, tiles_hbm, grad_hbm, stem_hbm, gain_ref, wqkv_hbm, wout_hbm, pos_ref) = refs[:8]
+    (scale_hbm, tiles_hbm, grad_hbm, stem_hbm, gain_hbm, wqkv_hbm, wout_hbm, pos_hbm) = refs[:8]
     (stem_out, gain_out, qkv_out, out_out) = refs[8:12]
     scratch = list(refs[12:])
     count = len(parts)
     nb = len(parts[0][1])
     first = [scratch.pop(0) for _ in range(count)]
-    recv = [[scratch.pop(0) for _ in range(nb)] for _ in range(count)]
+    recv = [[scratch.pop(0) for _ in range(nb - 1)] for _ in range(count)]
     send = [[None] + [scratch.pop(0) for _ in range(nb - 1)] for _ in range(count)]
     keep = [[scratch.pop(0) for _ in range(nb - 1)] for _ in range(count)]
-    (final, final_recv, stem_w, wqkv, wout, image, halo_rows, grad_pair, hidden_pair, attn_pair, dq_pair, dkv_pair,
+    (final, final_keep, last_in, stem_w, wqkv, wout, image, halo_rows, grad_pair, hidden_pair, attn_pair, dq_pair, dkv_pair,
      kv, dkv_out, dkv_own, dkv_in, dkv_mid, dkv_side, normed_ref, inv_ref, qk_ref, heads_inv, qn, da, attn, dq, dqkv,
-     tok_out, tok_all, stem_send, stem_got, stem_next, stem_last, gain_own, gain_got, gain_plane, gain_z, gain_col,
-     load_sem, pair_send, pair_got, final_send, final_got, halo_send, halo_got, tile_send, tile_got, pass_send, pass_got,
+     tok_out, tok_all, stem_send, stem_got, stem_next, stem_last, gain_own, gain_got, gain_plane, gain_z, gain_col, gain_ref, pos_ref, scale_ref,
+     load_sem, pair_send, pair_got, final_send, final_got, cross_got, halo_send, halo_got, tile_send, tile_got, pass_send, pass_got,
      kv_send, kv_got, dkv_send, dkv_got, part_send, part_got, tok_send, tok_got, gain_send, gain_arrived,
      gain_z_send, gain_z_got, stem_sent, stem_arrived) = scratch
     tok, width = grad_pair.shape[1:]
@@ -126,13 +126,16 @@
         pltpu.make_async_copy(wqkv_hbm, wqkv, load_sem.at[3]),
         pltpu.make_async_copy(grad_hbm, grad_pair.at[core], load_sem.at[4]),
         pltpu.make_async_copy(wout_hbm, wout, load_sem.at[5]),
+        pltpu.make_async_copy(gain_hbm, gain_ref, load_sem.at[6]),
+        pltpu.make_async_copy(pos_hbm, pos_ref, load_sem.at[7]),
+        pltpu.make_async_copy(scale_hbm, scale_ref, load_sem.at[8]),
     ]
     barrier = pltpu.get_barrier_semaphore()
     peers = [beside(i, j) for i, j in plane] + [level(k) for k in range(1, nz)] + [along(j) for j in (1, 2, 3, -1, -2, -3)]
     for peer in peers:
         pl.semaphore_signal(barrier, inc=1, device_id=peer, device_id_type=pl.DeviceIdType.MESH)
-    for load in loads:
-        load.start()
+    for which in (0, 1, 2, 6, 3, 4, 5, 7, 8):
+        loads[which].start()
     image[:, grid_count * tok :] = jnp.zeros((2, halo, pin), image.dtype)
 
     def push(source, target, sems, got, device):
@@ -154,9 +157,9 @@
         mine = image.at[own_x, own_rows]
         return push(mine, mine, tile_send.at[slot], tile_got.at[slot], beside(i, j))
 
+    pl.semaphore_wait(barrier, len(peers))
+    halo_copy = push(tiles_hbm.at[:halo], halo_rows, halo_send, halo_got, above)
     loads[0].wait()
-    pl.semaphore_wait(barrier, len(peers))
-    halo_copy = push(image.at[own_x, pl.ds(pl.multiple_of(own_grid * tok, tok), halo)], halo_rows, halo_send, halo_got, above)
     tile_copies = [tiles_to(0, 0, 2), tiles_to(1, 1, 0)]
     tile_pair = pair(0, image.at[own_x, own_rows], image.at[own_x, own_rows])
 
@@ -177,6 +180,7 @@
     normed = token_f * inv
     normed_ref[...] = normed
     inv_ref[...] = jnp.broadcast_to(inv, inv_ref.shape)
+    loads[6].wait()
     gain_f = gain_ref[...].astype(jnp.float32).reshape(1, width)
     hidden = (normed * gain_f).astype(jnp.bfloat16)
     hidden_pair[core] = hidden
@@ -225,6 +229,8 @@
     grad_own = grad_pair[core]
     da[...] = rowwise_dot(grad_own, wout[...]).astype(jnp.bfloat16)
 
+    loads[7].wait()
+    loads[8].wait()
     query_pos = pos_ref[pl.ds(own_blk, 1), :]
     seen = []
     for j in range(4):
@@ -242,8 +248,6 @@
     for g in range(KEY_VALUE_HEADS):
         kv_copy(g, 2, 0).wait_recv()
         kv_push(g, 2, 3 - 2 * own_x, 2, beside(1, 0))
-        if g > DIRECT_KEYS:
-            pass_up(g - 1)
 
     def dkv_push(source, g, slot, which, device):
         return push(source, dkv_in.at[g, slot], dkv_send.at[which], dkv_got.at[g, slot], device)
@@ -295,8 +299,7 @@
         dprobs = rowwise_dot(values_g, grads_g)
         probs, low = [], []
         for i in range(group):
-            s = jnp.where(visible, scores[:, i * tok : (i + 1) * tok] * scale_ref[g * group + i], -1e30)
-            weights = jnp.where(visible, jnp.exp(s - jnp.max(s, axis=0, keepdims=True)), 0.0)
+            weights = jnp.where(visible, jnp.exp(scores[:, i * tok : (i + 1) * tok] * scale_ref[g * group + i]), 0.0)
             p = weights * (1.0 / jnp.sum(weights, axis=0, keepdims=True))
             probs.append(p)
             low.append(p.astype(jnp.bfloat16))
@@ -320,11 +323,10 @@
             dkv_out[g, j - 1] = jnp.concatenate([dkeys[j], dvalues[j]], axis=1).astype(jnp.bfloat16)
         give(g)
         if g == 0:
-            pass_up(KEY_VALUE_HEADS - 1)
+            for h in range(DIRECT_KEYS, KEY_VALUE_HEADS):
+                pass_up(h)
         if 0 <= g - 1 < CHAINED:
             sideways(g - 1)
-        if g >= 2:
-            combine(g - 2)
     half = key_start // 2
 
     def half_of(start, amount, which):
@@ -345,6 +347,7 @@
 
     copies = [None] * count
     steps = [0] * count
+    held_back = [2, 5]
     starts = [sum(w for _, _, w in parts[:p]) for p in range(count)]
 
     def transfer(p, source):
@@ -358,7 +361,7 @@
             order, w = parts[p][1:]
             first[p][...] = product[:, at : at + w].reshape(first[p].shape)
             at += w
-            if order[0] < 2:
+            if p not in held_back:
                 launch(p)
 
     def launch(p):
@@ -368,6 +371,10 @@
     def advance(p):
         step, order = steps[p], parts[p][1]
         copies[p].wait_recv()
+        if step == nb - 1:
+            cols = slice(starts[p], starts[p] + parts[p][2])
+            final[:, cols] = keep[p][step - 1][core] + last_in[core, :, cols].astype(jnp.float32)
+            return
         held = recv[p][step]
         mine = chip_partner(order[step], own_blk, own_grid)[1]
         left_over = [b for b in range(nb) if b not in order[:step]]
@@ -379,17 +386,23 @@
             return keep[p][step - 1][i] + held[i].astype(jnp.float32)
 
         steps[p] = step + 1
-        if step == nb - 1:
-            value = total(0)
-            cols = slice(starts[p], starts[p] + parts[p][2])
-            final[0, :, cols] = value[:rows]
-            final[1, :, cols] = value[rows:]
-            push(final.at[1 - core, :, cols], final_recv.at[:, cols], final_send, final_got, other_core)
-            return
         left_over.remove(order[step])
         place_next = 1 << left_over.index(order[step + 1])
         mine_next = chip_partner(order[step + 1], own_blk, own_grid)[1]
         amount = 1 << (nb - 2 - step)
+        if amount == 1:
+            cols = slice(starts[p], starts[p] + parts[p][2])
+            gone, kept = total(1 - mine_next), total(mine_next)
+            partner = chip_partner(order[step + 1], own_blk, own_grid)[0]
+            across = {"blk": partner["blk"], "grid": other_core["grid"]}
+            for c in range(2):
+                send[p][step + 1][c] = gone[c * rows : (c + 1) * rows].astype(jnp.bfloat16)
+                keep[p][step][c] = kept[c * rows : (c + 1) * rows]
+            target = last_in.at[core, :, cols]
+            copies[p] = push(send[p][step + 1].at[core], target, part_send.at[step + 1], part_got.at[p, step + 1], partner)
+            push(send[p][step + 1].at[1 - core], target, part_send.at[step + 1], cross_got, across)
+            push(keep[p][step].at[1 - core], final_keep.at[:, cols], final_send, final_got, other_core)
+            return
         for r in range(amount):
             away = r // place_next * (2 * place_next) + (1 - mine_next) * place_next + r % place_next
             send[p][step + 1][r] = total(away).astype(jnp.bfloat16)
@@ -403,19 +416,23 @@
             advance(p)
 
     of_out, of_query, of_key = [[p for p in range(count) if parts[p][0] == m] for m in range(3)]
+    combine(0)
     attn_copy.wait()
     grad_copy.wait()
     begin(of_out, grad_pair[...], attn_pair[...].reshape(2 * tok, half))
-    for g in range(KEY_VALUE_HEADS - 2, KEY_VALUE_HEADS):
+    for g in (2, 1, 3):
         combine(g)
     launch(of_out[2])
+    dq_copy.wait()
+    hidden_copy.wait()
+    begin(of_query, hidden_pair[...], dq_pair[...].reshape(2 * tok, half))
+
     for slot, (i, j) in enumerate(((0, 2), (1, 0), (1, 2))):
         if slot != 1:
             tile_copies[slot].wait()
         where = image.at[(own_x + i) % 2, pl.ds(pl.multiple_of((own_grid + j) % grid_count * tok, tok), tok)]
         push(where, where, pass_send, pass_got, other_core)
 
-    advance_all(of_out[:2])
     for g in range(KEY_VALUE_HEADS):
         if g < CHAINED:
 
@@ -441,6 +458,7 @@
     dkv_copy = pair(5, dqkv.at[:, half_of(key_start, span, 1 - core)], dkv_pair.at[core])
     dkv_pair[core] = dqkv[:, half_of(key_start, span, core)]
     d_hidden = rowwise_dot(dqkv[...], wqkv[...])
+    advance_all(of_out[:2])
     normed = normed_ref[...]
     flow = d_hidden * gain_f
     inner_mean = jnp.sum(flow * normed, axis=1, keepdims=True) / width
@@ -459,13 +477,10 @@
         push(gain_own, gain_got.at[slot], gain_send, gain_arrived, beside(i, j))
     tok_all[own_x, :, own_lanes] = tok_out[own_x * grid_count + own_grid]
 
-    dq_copy.wait()
-    hidden_copy.wait()
-    begin(of_query, hidden_pair[...], dq_pair[...].reshape(2 * tok, half))
-
-    advance_all(of_out[:2])
+    launch(of_query[2])
     dkv_copy.wait()
     begin(of_key, hidden_pair[...], dkv_pair[...].reshape(2 * tok, span))
+    advance_all(of_out[:2])
     advance(of_out[2])
     tile_pair.wait()
     all_of(image.at[0, : 3 * tok], pass_send, pass_got).wait()
@@ -500,7 +515,9 @@
     advance_all(of_query + of_out + of_key)
     for h in range(chunks):
         stem_beyond(h)
-    advance_all(of_query + of_key + of_out[2:])
+        if h == chunks // 2 - 1:
+            advance_all(of_query)
+    advance_all(of_key + of_out[2:])
     advance_all(of_query + of_out[:2] + of_key + of_out[2:])
     advance_all(of_query)
     all_of(gain_z, gain_z_send, gain_z_got).wait()
@@ -518,7 +535,8 @@
         cols = slice(h * step, (h + 1) * step)
         stem_out[0, :, cols] = total[:rows]
         stem_out[1, :, cols] = total[rows:]
-    all_of(final.at[0], final_send, final_got).wait()
+    all_of(final_keep, final_send, final_got).wait()
+    all_of(last_in.at[0], final_send, cross_got).wait_recv()
     all_of(kv.at[:, 0], kv_send.at[0], final_got).wait_send()
     all_of(kv.at[:, 0], kv_send.at[2], final_got).wait_send()
 
@@ -538,7 +556,8 @@
         all_of(image.at[0, :amount], part_send.at[step], final_got).wait_send()
     all_of(stem_got, stem_sent.at[0], final_got).wait_send()
     all_of(stem_last, stem_sent.at[1], final_got).wait_send()
-    for source, which in ((final.at[core], core), (final_recv, 1 - core)):
+    final_keep[...] += last_in[1 - core].astype(jnp.float32)
+    for source, which in ((final, core), (final_keep, 1 - core)):
         out_out[:, half_of(0, half, which)] = source[:, :half]
         qkv_out[:, half_of(0, half, which)] = source[:, half : 2 * half]
         qkv_out[:, half_of(key_start, span, which)] = source[:, 2 * half :]
@@ -570,15 +589,17 @@
         firsts.append(((outer, 2, inner, rc, w), bf))
         recvs.append(((outer, inner, rc, w), bf))
         for step in range(1, nb):
-            shape = (1 << (nb - 1 - step), rc, w)
-            recvs.append((shape, bf))
+            shape = (1 << (nb - 1 - step), rc, w) if step < nb - 1 else (2, rows, w)
+            if step < nb - 1:
+                recvs.append((shape, bf))
             sends.append((shape, bf))
             keeps.append((shape, f32))
     total = sum(w for _, _, w in parts)
     chunks, heads = 4, KEY_VALUE_HEADS
     buffers = firsts + recvs + sends + keeps + [
-        ((2, rows, total), f32),
         ((rows, total), f32),
+        ((rows, total), f32),
+        ((2, rows, total), bf),
         (stem_weight.shape, bf),
         (w_qkv.shape, bf),
         (w_out.shape, bf),
@@ -615,10 +636,12 @@
         ((1, width), f32),
         ((nz - 1, 1, width), f32),
         ((width, 128), f32),
+        ((width,), bf),
+        ((blk_count, tok), positions.dtype),
     ]
     dma = pltpu.SemaphoreType.DMA
     count = len(parts)
-    semaphores = [dma((6,)), dma((6,)), dma((6,)), dma, dma, dma, dma, dma((3,)), dma((3,)), dma, dma]
+    semaphores = [dma((9,)), dma((6,)), dma((6,)), dma, dma, dma, dma, dma, dma((3,)), dma((3,)), dma, dma]
     semaphores += [dma((4,)), dma((heads, 4)), dma((3,)), dma((heads, 4)), dma((nb,)), dma((count, nb))]
     semaphores += [dma] * 6 + [dma((2,)), dma((chunks, 2))]
     vmem = pl.BlockSpec(memory_space=pltpu.VMEM)
@@ -631,9 +654,9 @@
     results = pl.pallas_call(
         partial(layer_kernel, (nz, parts)),
         out_shape=shapes,
-        in_specs=[pl.BlockSpec(memory_space=pltpu.SMEM), hbm, hbm, hbm, vmem, hbm, hbm, vmem],
+        in_specs=[hbm] * 8,
         out_specs=[vmem] * 4,
-        scratch_shapes=[pltpu.VMEM(shape, kind) for shape, kind in buffers] + semaphores,
+        scratch_shapes=[pltpu.VMEM(shape, kind) for shape, kind in buffers] + [pltpu.SMEM(per_head_scale.shape, f32)] + semaphores,
         compiler_params=pltpu.CompilerParams(collective_id=0, has_side_effects=True, vmem_limit_bytes=56000000),
     )(*[pltpu.with_memory_space_constraint(value, pltpu.HBM) for value in inputs])
     return pl.pallas_call(

time: 60.7 us -> 57.1 us (0.941)
  Pallas kernels: 59.9 us -> 56.3 us
    pallas_call x1, Pallas kernels: 59.2 us -> 55.6 us  [whole_layer(): pl.pallas_call(partial(layer_kernel, (nz, parts)), out_shape=shapes, in_s...]
where the time goes in v4:
time: 57.1 us; the launch traced here: 57 us
  Pallas kernels  56.3 us (99%)
  between operations  0.64 us (1%)
    pallas_call x1, Pallas kernels, whole_layer(): pl.pallas_call(partial(layer_kernel, (nz, parts)), out_shape=shapes, in_s...  55.6 us

profile of v4, /device:TPU:0, one launch (start us, length us, event | category | flops | bytes accessed | tf_op | source)
XLA Modules:
  0.0 57.0 jit_solution(9936540020664752940)
XLA Ops:
  0.6 55.6 %shard_map.111 = (f32[2,24,1024]{2,1,0:T(8,128)S(1)}, f32[1,24]{1,0:T(1,128)S(1)}, f32[24,1280]{1,0:T(8,128)S(1)}, f32[24,768]{1,0:T(8,128)S(1)}) custom-call(f32[12]{0:T(128)} %refs_0_.1, bf16[128,1024]{1,0:T(8,128)(2,1)} %bitcast.6, bf16[128,768]{1,0:T(8,128)(2,1)} %bitcast.7, bf16[2,1024,768]{2,1,0:T(8,128)(2,1)} %refs_3_.1, bf16[768]{0:T(1024)(128)(2,1)} %refs_4_.1, ...), custom_call_target="tpu_custom_call" | custom-call | tf_op jit(solution)/shard_map/pallas_call | solution.py:654
  56.2 0.8 %shard_map.112 = (f32[2,24,1024]{2,1,0:T(8,128)}, f32[1,24]{1,0:T(1,128)}, f32[24,1280]{1,0:T(8,128)}, f32[24,768]{1,0:T(8,128)}) custom-call(f32[2,24,1024]{2,1,0:T(8,128)S(1)} %get-tuple-element.12.refs_0_, f32[1,24]{1,0:T(1,128)S(1)} %get-tuple-element.13.refs_1_, f32[24,1280]{1,0:T(8,128)S(1)} %get-tuple-element.14.refs_2_, ...), custom_call_target="tpu_custom_call" | custom-call | tf_op jit(solution)/shard_map/pallas_call | solution.py:662
